TPU v7x, 32 devices: a whole 2x2x4 slice. The times are simulated.
32 devices in a mesh: ctx: 8 (over z, core), inner: 4 (over y, x).
Axes of the slice: x: 2, y: 2, z: 4, core: 2. Of those that a mesh axis runs over, the one named last changes fastest.
Arguments:
- tokens: bfloat16 [4096, 2048], P(('ctx', 'inner')), may hold values from -6 to 6
- project_weight: bfloat16 [2048, 2, 4096], P('ctx', None, 'inner'), may hold values from -0.125 to 0.125
- state_weight: bfloat16 [2048, 2, 512], P('ctx', None, 'inner'), may hold values from -0.125 to 0.125
- step_weight: bfloat16 [2048, 64], P('ctx', 'inner'), may hold values from -0.125 to 0.125
- mixer_taps: float32 [5, 4096], P(None, 'inner'), may hold values from -2.5 to 2.5
- state_taps: float32 [5, 2, 512], replicated, may hold values from -2.5 to 2.5
- step_bias: float32 [64], P('inner'), may hold values from -4.6 to -2.3
- decay_log: float32 [64], P('inner'), may hold values from -13 to 0.5, as said below
- norm_gain: float32 [4096], replicated, may hold values from 0.1 to 1.9
Outputs:
- mixed_output: bfloat16 [4096, 4096], P(('ctx', 'inner'))
Inputs may be any that keep to these rules, and one draw needn't show every extreme that they name: `decay_log`: one value a head.
All inputs are finite; a program needn't handle non-finite values.
Results may differ from a plain program's by a relative error of at most 0.0075.
Values may be sent and summed in bfloat16 or wider, within the bound.
No kernel may reach another device: no remote copies, remote signals or barrier semaphores. Data moves between devices by JAX's collectives and lax.ppermute only.
A program may use at most 64 MiB of HBM per device.

v0:
```python
import jax
import jax.numpy as jnp
from jax import lax
from jax.experimental import pallas as pl
from jax.experimental.pallas import tpu as pltpu
from jax.sharding import PartitionSpec as P


H = 64
P_SIZE = 64
N = 128
G = 4
CONV = 4
SPAN = 128
TEAM = 4
HALO = 16
LANES = 128
PAD = 8

EPSILON = 1e-05


ANY = pl.BlockSpec(memory_space=pl.ANY)
VMEM = pl.BlockSpec(memory_space=pltpu.VMEM)
SMEM = pl.BlockSpec(memory_space=pltpu.SMEM)
SMALL = pltpu.CompilerParams(vmem_limit_bytes=6 << 20)
F32 = jnp.float32
BF16 = jnp.bfloat16


def swapped(x, axis, mask):
    pairs = [(i, i ^ mask) for i in range(lax.axis_size(axis))]
    return lax.ppermute(x, axis, pairs)


def inner_blocks(block, place, inner_count, ctx_count):
    if inner_count != 4:
        got = [block]
        step = 1
        while step < inner_count:
            got = got + [swapped(b, "inner", step) for b in got]
            step *= 2
        return got
    near_x = swapped(block, "inner", 1)
    near_y = swapped(block, "inner", 2)
    pairs = []
    for c in range(ctx_count):
        for i in range(inner_count):
            pairs.append((c * inner_count + i, c * inner_count + (i ^ (1 if c % 2 else 2))))
    onward = pl.pallas_call(
        either_kernel,
        in_specs=[SMEM, ANY, ANY],
        out_specs=VMEM,
        out_shape=jax.ShapeDtypeStruct(block.shape, block.dtype),
        scratch_shapes=[pltpu.SemaphoreType.DMA],
        compiler_params=SMALL,
        name="either",
    )(place, near_x, near_y)
    far = lax.ppermute(onward, ("ctx", "inner"), pairs)
    return [block, near_x, near_y, far]


def gathered_rows(piece_of, z_count):
    return [piece_of(d) if d == 0 else swapped(piece_of(d), "ctx", 2 * d) for d in range(z_count)]


def fetch_weights(place, parts, scratch, sems):
    z_id, core = place[2], place[3]
    copies = []
    for index, (view, d, m) in enumerate(parts):
        rows = view.shape[0]
        row = pl.multiple_of((2 * (z_id ^ d) + (core ^ m)) * rows, rows)
        copies.append(pltpu.make_async_copy(view, scratch.at[pl.ds(row, rows)], sems.at[index]))
    for copy in copies:
        copy.start()
    return copies


def prepare_kernel(heads_mine, place, project, state, step, taps, mixer_taps, step_bias, decay_log, *outs):
    x_same, x_opposite, gate_same, gate_opposite, gate_sent, state_turned, step_same, step_opposite, taps_state = outs[:9]
    taps_mixer, bias, rate = outs[9:]
    side, core = place[4], place[3]
    pair = x_same.shape[1]
    width = pair // 2

    def columns(kind, index, size):
        if size % LANES == 0:
            return project[:, kind, pl.ds(pl.multiple_of(index * size, size), size)]
        got = project[:, kind, :size]
        for k in range(1, project.shape[2] // size):
            got = jnp.where(index == k, project[:, kind, k * size : (k + 1) * size], got)
        return got

    other_side = 1 - side
    x_same[...] = columns(1, side, pair)
    x_opposite[...] = columns(1, other_side, pair)
    gate_same[...] = columns(0, 2 * side + core, width)
    gate_opposite[...] = columns(0, 2 * other_side + core, width)
    gate_sent[:, :width] = columns(0, 2 * side + 1 - core, width)
    gate_sent[:, width:] = columns(0, 2 * other_side + 1 - core, width)
    cols = state.shape[2]
    target = lax.broadcasted_iota(jnp.int32, (2 * cols, cols), 0)
    source = lax.broadcasted_iota(jnp.int32, (2 * cols, cols), 1)
    per = cols // G
    turned = 0.0
    for part in range(2):
        wanted = (source % G) * 2 * per + part * per + source // G
        turned = turned + lax.dot_general(
            (target == wanted).astype(BF16),
            state[:, part, :],
            (((1,), (1,)), ((), ())),
            preferred_element_type=F32,
        )
    state_turned[...] = turned.astype(BF16)
    heads = step.shape[1]
    rows = step.shape[0]
    wide = jnp.concatenate([step[...].astype(F32), jnp.zeros((rows, LANES - heads), F32)], axis=1)
    turned_step = wide.T[: 2 * PAD]
    half = heads // 2
    low = turned_step[:PAD]
    high = turned_step[half : half + PAD]
    step_same[...] = jnp.where(side == 0, low, high).astype(BF16)
    step_opposite[...] = jnp.where(side == 0, high, low).astype(BF16)
    source = lax.broadcasted_iota(jnp.int32, (taps.shape[2], N), 0)
    target = lax.broadcasted_iota(jnp.int32, (taps.shape[2], N), 1)
    chosen = (source == target * G + place[5]).astype(F32)
    mine = jnp.where(core == 0, taps[:, 0, :], taps[:, 1, :])
    taps_state[: CONV + 1] = exact_dot(mine, chosen, ((1,), (0,)))
    quarter = place[0]
    if width % LANES == 0:
        taps_mixer[: CONV + 1] = mixer_taps[:, pl.ds(pl.multiple_of(quarter * width, width), width)]
    else:
        got = mixer_taps[:, :width]
        for k in range(1, TEAM):
            got = jnp.where(quarter == k, mixer_taps[:, k * width : (k + 1) * width], got)
        taps_mixer[: CONV + 1] = got
    row = lax.broadcasted_iota(jnp.int32, (PAD, heads), 0)
    column = lax.broadcasted_iota(jnp.int32, (PAD, heads), 1)
    own = jnp.logical_and(column == quarter * heads_mine + row, row < heads_mine)
    for values, out in ((step_bias[...], bias), (-jnp.exp(decay_log[...]), rate)):
        picked = jnp.sum(jnp.where(own, values, 0.0), axis=1, keepdims=True)
        out[...] = jnp.broadcast_to(picked, out.shape)


def either_kernel(place, first, second, out, sem):
    for core, values in enumerate((first, second)):

        @pl.when(place[3] == core)
        def _():
            copy = pltpu.make_async_copy(values, out, sem)
            copy.start()
            copy.wait()


def partner_columns_kernel(place, *refs):
    pieces, out = refs[:-1], refs[-1]
    width = out.shape[2]
    other = 1 - place[3]
    for d, piece in enumerate(pieces):
        if width % LANES == 0:
            out[d] = piece[:, pl.ds(pl.multiple_of(other * width, width), width)]
        else:
            out[d] = jnp.where(other == 0, piece[:, :width], piece[:, width:])


def partner_rows_kernel(place, *refs):
    pieces, out = refs[:-1], refs[-1]
    other = pl.multiple_of((1 - place[3]) * N, N)
    for d, piece in enumerate(pieces):
        out[d, :N] = piece[pl.ds(other, N), :]
        out[d, N:] = piece[2 * N :, :]


def payload_kernel(place, turned, *refs):
    received, steps, outs = refs[:-4], refs[-4:-2], refs[-2:]
    inner_id = place[1]
    rows = turned.shape[0] // G
    part = rows // 2
    for d in range(len(received) + 1):
        piece = received[d - 1] if d else turned.at[pl.ds(pl.multiple_of(place[5] * rows, rows), rows)]
        for k in range(2):
            start = pl.multiple_of(k * N + (inner_id ^ d) * part, part)
            for out in outs:
                out[pl.ds(start, part), :] = piece[k * part : (k + 1) * part, :]
    for step, out in zip(steps, outs):
        out[2 * N :, :] = step[...]


def sent_kernel(group_of, place, turned, *outs):
    rows = turned.shape[0] // G
    for d, out in enumerate(outs):
        start = pl.multiple_of(group_of(place[1] ^ (d + 1)) * rows, rows)
        out[...] = turned[pl.ds(start, rows), :]


def assemble_kernel(heads_mine, place, sent, *refs):
    pieces, out = refs[:-1], refs[-1]
    z_id, core = place[2], place[3]
    rows = pieces[0].shape[1]
    for d, piece in enumerate(pieces):
        own = piece[pl.ds(pl.multiple_of(core * N, N), N), :]
        for m, (state, step) in enumerate(((own, piece[2 * N :, :]), (sent[d, :N, :], sent[d, N:, :]))):
            step = step.astype(F32)
            mine = jnp.where(core == 0, step[:heads_mine], step[heads_mine : 2 * heads_mine])
            packed = jnp.concatenate(
                [state.astype(F32), mine, jnp.zeros((LANES - heads_mine, rows), F32)], axis=0
            )
            row = pl.multiple_of((2 * (z_id ^ d) + (core ^ m)) * rows, rows)
            out[pl.ds(row, rows), :] = packed.T.astype(BF16)


def tail_kernel(place, *refs):
    blocks, out, sem = refs[:-2], refs[-2], refs[-1]
    last = len(blocks) - 1
    for d, block in enumerate(blocks):

        @pl.when(place[1] == (last ^ d))
        def _():
            copy = pltpu.make_async_copy(block.at[pl.ds(block.shape[0] - HALO, HALO)], out, sem)
            copy.start()
            copy.wait()


def fetch_blocks(place, blocks, scratch, sems, inner_count, offset):
    inner_id = place[1]
    rows = blocks[0].shape[0]
    copies = []
    for d, block in enumerate(blocks):
        j, di = d // inner_count, d % inner_count
        row = pl.multiple_of(offset + j * inner_count * rows + (inner_id ^ di) * rows, HALO)
        copies.append(pltpu.make_async_copy(block, scratch.at[pl.ds(row, rows)], sems.at[d]))
    for copy in copies:
        copy.start()
    return copies


def wide_dot(a, b):
    return jnp.dot(a, b, preferred_element_type=F32)


def exact_dot(a, b, dims):
    return lax.dot_general(a, b, (dims, ((), ())), precision=lax.Precision.HIGHEST, preferred_element_type=F32)


def convolved(pre, taps, block):
    window = pre[pl.ds(pl.multiple_of(block * SPAN, SPAN), SPAN + HALO), :].astype(F32)
    start = HALO - (CONV - 1)
    mixed = taps[CONV : CONV + 1, :] + taps[0:1, :] * window[start : start + SPAN]
    for k in range(1, CONV):
        mixed = mixed + taps[k : k + 1, :] * window[start + k : start + k + SPAN]
    return mixed / (1.0 + jnp.exp(-mixed))


def spread(width):
    row = lax.broadcasted_iota(jnp.int32, (PAD, width), 0)
    column = lax.broadcasted_iota(jnp.int32, (PAD, width), 1)
    return (column // P_SIZE == row).astype(F32)


def projected(place, source, parts, tok, weight, sems, wsems, inner_count, keep):
    waits = fetch_weights(place, parts, weight, wsems) if parts else []
    blocks = source[:-1]
    span = (tok.shape[0] - HALO) // TEAM
    copies = []
    if blocks:
        top = pltpu.make_async_copy(source[-1], tok.at[pl.ds(0, HALO)], sems.at[len(blocks)])
        top.start()
        copies = fetch_blocks(place, blocks, tok, sems, inner_count, HALO)
        waits = waits + [top]
    for copy in waits:
        copy.wait()
    for j in range(TEAM):
        for di in range(inner_count if blocks else 0):
            copies[j * inner_count + di].wait()
        first = 0 if j == 0 else HALO + j * span
        size = span + (HALO if j == 0 else 0)
        keep(wide_dot(tok[pl.ds(first, size), :], weight[...]), j)


def state_kernel(inner_count, place, taps, bias, rate, weight, *refs):
    source, refs = refs[:-6], refs[-6:]
    half_out, step_out, cum_out, tok, pre, sems = refs
    span = (tok.shape[0] - HALO) // TEAM
    quarter = place[0]

    def keep(result, j):
        if j == 0:
            pre[pl.ds(0, HALO), :] = result[:HALO, :N].astype(BF16)
            result = result[HALO:]
        whose = quarter ^ j
        pre[pl.ds(pl.multiple_of(HALO + whose * span, HALO), span), :] = result[:, :N].astype(BF16)
        raw = result[:, N:].astype(BF16).astype(F32)
        for b in range(span // SPAN):
            turned = raw[b * SPAN : (b + 1) * SPAN].T
            step_out[whose * (span // SPAN) + b] = turned[:PAD]

    projected(place, source, (), tok, weight, sems, None, inner_count, keep)

    total = step_out.shape[0] * PAD
    raw = step_out[...] + bias[...][None]
    step = jnp.maximum(raw, 0.0) + jnp.log1p(jnp.exp(-jnp.abs(raw)))
    step_out[...] = step
    logdec = (step * rate[...][None]).reshape(total, SPAN)
    row = lax.broadcasted_iota(jnp.int32, (SPAN, SPAN), 0)
    column = lax.broadcasted_iota(jnp.int32, (SPAN, SPAN), 1)
    upper = (row <= column).astype(F32)
    cum_out[...] = exact_dot(logdec, upper, ((1,), (0,))).reshape(step_out.shape)

    def one(p, _):
        half_out[pl.ds(pl.multiple_of(p * SPAN, SPAN), SPAN), :] = convolved(pre, taps, p).astype(BF16)
        return 0

    lax.fori_loop(0, step_out.shape[0], one, 0, unroll=2)


def mixer_kernel(inner_count, shared, z_count, place, taps, half, half_other, step, cum, other, *refs):
    pieces, refs = refs[:z_count], refs[z_count:]
    tail = 8 if shared else 9
    source, refs = refs[:-tail], refs[-tail:]
    if shared:
        tok, source = source[0], ()
        x_out, states_out, last_out, through_out, weight, pre, sems, wsems = refs
        source = (None,)
    else:
        x_out, states_out, last_out, through_out, tok, weight, pre, sems, wsems = refs
    span = (tok.shape[0] - HALO) // TEAM
    quarter, core = place[0], place[3]
    width = x_out.shape[1]
    parts = []
    for d, piece in enumerate(pieces):
        view = piece
        if piece.shape[1] != width:
            view = piece.at[:, pl.ds(pl.multiple_of(core * width, width), width)]
        parts += [(view, d, 0), (other.at[d], d, 1)]

    def keep(result, j):
        if j == 0:
            pre[pl.ds(0, HALO), :] = result[:HALO].astype(BF16)
            result = result[HALO:]
        whose = quarter ^ j
        pre[pl.ds(pl.multiple_of(HALO + whose * span, HALO), span), :] = result.astype(BF16)

    projected(place, source, parts, tok, weight, sems, wsems, inner_count, keep)
    heads = spread(width)

    def one(p, carry):
        state, log_sum = carry
        rows = pl.ds(pl.multiple_of(p * SPAN, SPAN), SPAN)
        x = convolved(pre, taps, p).astype(BF16)
        x_out[rows, :] = x
        states_out[p] = state
        cum_p = cum[p]
        ends = cum_p[:, SPAN - 1 :]
        to_end = jnp.exp(ends - cum_p) * step[p]
        scaled = (x.astype(F32) * exact_dot(to_end, heads, ((0,), (0,)))).astype(BF16)
        b = jnp.where(core == 0, half[rows, :], half_other[rows, :])
        fresh = lax.dot_general(b, scaled, (((0,), (0,)), ((), ())), preferred_element_type=F32)
        end_row = jnp.sum(ends * heads, axis=0, keepdims=True)
        return jnp.exp(end_row) * state + fresh, log_sum + end_row

    state, log_sum = lax.fori_loop(
        0, step.shape[0], one, (jnp.zeros((N, width), F32), jnp.zeros((1, width), F32)), unroll=2
    )
    last_out[...] = state.astype(BF16)
    through_out[...] = jnp.broadcast_to(jnp.exp(log_sum), through_out.shape)


def gate_kernel(inner_count, shared, z_count, place, *refs):
    pieces, refs = refs[:z_count], refs[z_count:]
    tail = 4 if shared else 5
    source, refs = refs[:-tail], refs[-tail:]
    if shared:
        tok = source[0]
        source = (None,)
        gate_out, weight, sems, wsems = refs
    else:
        gate_out, tok, weight, sems, wsems = refs
    span = (tok.shape[0] - HALO) // TEAM
    quarter = place[0]
    parts = []
    for d, piece in enumerate(pieces):
        rows = piece.shape[0] // 2
        parts += [(piece.at[pl.ds(m * rows, rows)], d, m) for m in range(2)]

    def keep(result, j):
        result = result[HALO:] if j == 0 else result
        gate_out[pl.ds(pl.multiple_of((quarter ^ j) * span, span), span), :] = result.astype(BF16)

    projected(place, source, parts, tok, weight, sems, wsems, inner_count, keep)


def scan_kernel(place, half, half_other, x_vals, gate, step, cum, states, prior, gated_out):
    width = x_vals.shape[1]
    heads_mine = width // P_SIZE
    heads = spread(width)
    core = place[3]
    lane = lax.broadcasted_iota(jnp.int32, (SPAN, width), 1) // P_SIZE
    row = lax.broadcasted_iota(jnp.int32, (SPAN, SPAN), 0)
    column = lax.broadcasted_iota(jnp.int32, (SPAN, SPAN), 1)
    lower = column <= row
    entering = prior[...].astype(F32)

    def one(p, before):
        rows = pl.ds(pl.multiple_of(p * SPAN, SPAN), SPAN)
        first, second = half[rows, :], half_other[rows, :]
        b = jnp.where(core == 0, first, second)
        c = jnp.where(core == 0, second, first)
        x = x_vals[rows, :]
        cum_p = cum[p]
        step_p = step[p]
        scores = lax.dot_general(
            c, b, (((1,), (1,)), ((), ())), preferred_element_type=F32
        )
        cum_t = cum_p.T
        mixes = []
        parts = []
        for h in range(heads_mine):
            spacing = jnp.where(lower, cum_t[:, h : h + 1] - cum_p[h : h + 1, :], -jnp.inf)
            mixes.append((scores * jnp.exp(spacing) * step_p[h : h + 1, :]).astype(BF16))
            parts.append(jnp.where(lane == h, x, jnp.zeros_like(x)))
        diagonal = wide_dot(jnp.concatenate(mixes, axis=1), jnp.concatenate(parts, axis=0))
        state = states[p] + jnp.exp(before) * entering
        decay = exact_dot(jnp.exp(cum_p), heads, ((0,), (0,)))
        y = diagonal + decay * wide_dot(c, state.astype(BF16))
        g = gate[rows, :].astype(F32)
        gated_out[rows, :] = (y * (g / (1.0 + jnp.exp(-g)))).astype(BF16)
        return before + jnp.sum(cum_p[:, SPAN - 1 :] * heads, axis=0, keepdims=True)

    lax.fori_loop(0, step.shape[0], one, jnp.zeros((1, width), F32), unroll=2)


def norm_kernel(inner_count, parts, gain, out):
    width = parts.shape[2]
    group_width = H * P_SIZE // G
    for g in range(G):
        members = []
        power = 0.0
        for c in range(g * group_width, (g + 1) * group_width, width):
            index = c // width
            i, k = index // TEAM, index % TEAM
            wide = parts[k * inner_count + i].astype(F32)
            members.append((c, wide))
            power = power + jnp.sum(wide * wide, axis=1, keepdims=True)
        scale = lax.rsqrt(power / group_width + EPSILON)
        for c, wide in members:
            out[:, c : c + width] = (wide * scale * gain[:, c : c + width]).astype(BF16)


def on_device(
    tokens,
    project_weight,
    state_weight,
    step_weight,
    mixer_taps,
    state_taps,
    step_bias,
    decay_log,
    norm_gain,
):
    ctx_count = lax.axis_size("ctx")
    inner_count = lax.axis_size("inner")
    ctx_id = lax.axis_index("ctx")
    inner_id = lax.axis_index("inner")
    core = ctx_id % 2
    z_id = ctx_id // 2
    z_count = ctx_count // 2
    side = z_id % 2
    quarter = ctx_id % TEAM
    members = TEAM * inner_count

    rows_here, _, width_here = project_weight.shape
    row_count, model_width = tokens.shape
    heads_here = step_weight.shape[1]
    heads_mine = heads_here // TEAM
    width_mine = width_here // TEAM
    per_group = H // G
    group = inner_id * heads_here // per_group
    place = jnp.stack([quarter, inner_id, z_id, core, side, group]).astype(jnp.int32)
    total = members * row_count
    count = total // SPAN

    def sds(shape, dtype):
        return jax.ShapeDtypeStruct(shape, dtype)

    partner = swapped(tokens, "ctx", 2)
    near = inner_blocks(tokens, place, inner_count, ctx_count)
    beyond = inner_blocks(partner, place, inner_count, ctx_count)
    blocks = (
        near
        + [swapped(b, "ctx", 1) for b in near]
        + beyond
        + [swapped(b, "ctx", 1) for b in beyond]
    )
    tail = pl.pallas_call(
        tail_kernel,
        in_specs=[SMEM] + [ANY] * len(near),
        out_specs=VMEM,
        out_shape=sds((HALO, model_width), BF16),
        scratch_shapes=[pltpu.SemaphoreType.DMA],
        compiler_params=SMALL,
        name="tail",
    )(place, *near)
    halo = jnp.zeros_like(tail)
    for k in range(TEAM):
        pairs = [(c - 1, c + k) for c in range(TEAM, ctx_count, TEAM)]
        halo = halo + lax.ppermute(tail, "ctx", pairs)

    pair = 2 * width_mine
    slice_cols = state_weight.shape[2]
    prepared = pl.pallas_call(
        lambda *refs: prepare_kernel(heads_mine, *refs),
        in_specs=[SMEM] + [VMEM] * 7,
        out_specs=[VMEM] * 12,
        out_shape=[
            sds((rows_here, pair), BF16),
            sds((rows_here, pair), BF16),
            sds((rows_here, width_mine), BF16),
            sds((rows_here, width_mine), BF16),
            sds((rows_here, pair), BF16),
            sds((2 * slice_cols, rows_here), BF16),
            sds((PAD, rows_here), BF16),
            sds((PAD, rows_here), BF16),
            sds((PAD, N), F32),
            sds((PAD, width_mine), F32),
            sds((PAD, SPAN), F32),
            sds((PAD, SPAN), F32),
        ],
        compiler_params=SMALL,
        name="prepare",
    )(
        place,
        project_weight,
        state_weight,
        step_weight,
        state_taps,
        mixer_taps,
        step_bias.reshape(1, -1),
        decay_log.reshape(1, -1),
    )
    x_sides, gate_mine, gate_sent = prepared[0:2], prepared[2:4], prepared[4]
    state_turned, step_sides = prepared[5], prepared[6:8]

    x_pieces = gathered_rows(lambda d: x_sides[d % 2], z_count)

    def of_core(piece, which):
        return lax.dynamic_slice_in_dim(piece, which * width_mine, width_mine, 1)

    x_sent = pl.pallas_call(
        partner_columns_kernel,
        in_specs=[SMEM] + [VMEM] * z_count,
        out_specs=VMEM,
        out_shape=sds((z_count, rows_here, width_mine), BF16),
        compiler_params=SMALL,
        name="xsplit",
    )(place, *x_pieces)
    x_other = swapped(x_sent, "ctx", 1)
    if width_mine % LANES:
        x_pieces = [of_core(p, core) for p in x_pieces]

    part_rows = 2 * slice_cols // G
    if part_rows % (2 * HALO) == 0:
        sent = pl.pallas_call(
            lambda *refs: sent_kernel(lambda j: j * heads_here // per_group, *refs),
            in_specs=[SMEM, VMEM],
            out_specs=[VMEM] * (inner_count - 1),
            out_shape=[sds((part_rows, rows_here), BF16)] * (inner_count - 1),
            compiler_params=SMALL,
            name="sent",
        )(place, state_turned)
        received = [swapped(sent[d - 1], "inner", d) for d in range(1, inner_count)]
        payloads = pl.pallas_call(
            payload_kernel,
            in_specs=[SMEM] + [VMEM] * (inner_count + 2),
            out_specs=[VMEM] * 2,
            out_shape=[sds((2 * N + PAD, rows_here), BF16)] * 2,
            compiler_params=SMALL,
            name="payload",
        )(place, state_turned, *received, *step_sides)
    else:
        to_each = jnp.concatenate(
            [
                lax.slice_in_dim(state_turned, g * part_rows, (g + 1) * part_rows, axis=0)
                for g in [(j * heads_here) // per_group for j in range(inner_count)]
            ],
            axis=0,
        ).reshape(inner_count, part_rows, rows_here)
        state_rows = lax.all_to_all(to_each, "inner", 0, 0, tiled=True)
        state_rows = state_rows.reshape(inner_count, 2, part_rows // 2, rows_here)
        state_rows = state_rows.transpose(1, 0, 2, 3).reshape(2 * N, rows_here)
        payloads = [jnp.concatenate([state_rows, s], axis=0) for s in step_sides]
    state_pieces = gathered_rows(lambda d: payloads[d % 2], z_count)
    state_sent = pl.pallas_call(
        partner_rows_kernel,
        in_specs=[SMEM] + [VMEM] * z_count,
        out_specs=VMEM,
        out_shape=sds((z_count, N + PAD, rows_here), BF16),
        compiler_params=SMALL,
        name="ssplit",
    )(place, *state_pieces)
    state_other = swapped(state_sent, "ctx", 1)
    state_matrix = pl.pallas_call(
        lambda *refs: assemble_kernel(heads_mine, *refs),
        in_specs=[SMEM] + [VMEM] * (1 + z_count),
        out_specs=VMEM,
        out_shape=sds((model_width, N + LANES), BF16),
        compiler_params=SMALL,
        name="assemble",
    )(place, state_other, *state_pieces)

    gate_other = swapped(gate_sent, "ctx", 1)
    gate_chip = [
        jnp.concatenate([gate_mine[s], gate_other[:, s * width_mine : (s + 1) * width_mine]], axis=0)
        for s in range(2)
    ]
    gate_pieces = gathered_rows(lambda d: gate_chip[d % 2], z_count)

    taps_state, taps_mine, bias_mine, rate_mine = prepared[8:]

    shared = total * model_width <= 2**23
    tok_shape = (HALO + total, model_width)
    held = 2 * tok_shape[0] * model_width
    limit = pltpu.CompilerParams(vmem_limit_bytes=min(60 << 20, held + (4 << 20 if shared else 22 << 20)))

    def scratch(width, pre_width, own_tok):
        made = [pltpu.VMEM(tok_shape, BF16)] if own_tok else []
        if width:
            made.append(pltpu.VMEM((model_width, width), BF16))
        if pre_width:
            made.append(pltpu.VMEM((HALO + total, pre_width), BF16))
        return made + [pltpu.SemaphoreType.DMA((members + 1,)), pltpu.SemaphoreType.DMA((2 * z_count,))]

    source = list(blocks) + [halo]
    any_of = lambda values: [ANY] * len(values)
    state_outs = [sds((total, N), BF16), sds((count, PAD, SPAN), F32), sds((count, PAD, SPAN), F32)]
    outs = pl.pallas_call(
        lambda *refs: state_kernel(inner_count, *refs),
        in_specs=[SMEM, VMEM, VMEM, VMEM, VMEM] + any_of(source),
        out_specs=[VMEM] * (4 if shared else 3),
        out_shape=state_outs + ([sds(tok_shape, BF16)] if shared else []),
        scratch_shapes=scratch(0, N, not shared)[:-1],
        compiler_params=limit,
        name="state",
    )(place, taps_state, bias_mine, rate_mine, state_matrix, *source)
    half, step, cum = outs[:3]
    if shared:
        source = [outs[3]]
    held_spec = [VMEM] if shared else any_of(source)
    half_other = swapped(half, "ctx", 1)

    x_vals, states, last_state, through = pl.pallas_call(
        lambda *refs: mixer_kernel(inner_count, shared, z_count, *refs),
        in_specs=[SMEM, VMEM, VMEM, VMEM, VMEM, VMEM, ANY] + any_of(x_pieces) + held_spec,
        out_specs=[VMEM, VMEM, VMEM, VMEM],
        out_shape=[
            sds((total, width_mine), BF16),
            sds((count, N, width_mine), F32),
            sds((N, width_mine), BF16),
            sds((PAD, width_mine), F32),
        ],
        scratch_shapes=scratch(width_mine, width_mine, not shared),
        compiler_params=limit,
        name="mixer",
    )(place, taps_mine, half, half_other, step, cum, x_other, *x_pieces, *source)

    hops = ctx_count // TEAM - 1
    pairs = [(c, c + TEAM) for c in range(ctx_count - TEAM)]
    prior = jnp.zeros_like(last_state)
    for hop in range(hops):
        sent = last_state
        if hop:
            sent = (through[:1] * prior.astype(F32) + last_state.astype(F32)).astype(BF16)
        prior = lax.ppermute(sent, "ctx", pairs)

    gate_values = pl.pallas_call(
        lambda *refs: gate_kernel(inner_count, shared, z_count, *refs),
        in_specs=[SMEM] + any_of(gate_pieces) + held_spec,
        out_specs=VMEM,
        out_shape=sds((total, width_mine), BF16),
        scratch_shapes=scratch(width_mine, 0, not shared),
        compiler_params=limit,
        name="gate",
    )(place, *gate_pieces, *source)

    gated = pl.pallas_call(
        scan_kernel,
        in_specs=[SMEM] + [VMEM] * 8,
        out_specs=VMEM,
        out_shape=sds((total, width_mine), BF16),
        compiler_params=limit,
        name="scan",
    )(place, half, half_other, x_vals, gate_values, step, cum, states, prior)

    teams = [[t * members + m for m in range(members)] for t in range(ctx_count // TEAM)]
    parts = lax.all_to_all(
        gated, ("ctx", "inner"), 0, 0, axis_index_groups=teams, tiled=True
    ).reshape(members, row_count, width_mine)
    return pl.pallas_call(
        lambda *refs: norm_kernel(inner_count, *refs),
        in_specs=[VMEM, VMEM],
        out_specs=VMEM,
        out_shape=sds((row_count, H * P_SIZE), BF16),
        compiler_params=limit,
        name="norm",
    )(parts, norm_gain.reshape(1, -1))


def solution(mesh):
    placed = (
        P(("ctx", "inner"), None),
        P("ctx", None, "inner"),
        P("ctx", None, "inner"),
        P("ctx", "inner"),
        P(None, "inner"),
        P(),
        P("inner"),
        P("inner"),
        P(),
    )

    return jax.shard_map(
        on_device, mesh=mesh, in_specs=placed, out_specs=P(("ctx", "inner"), None), check_vma=False
    )
```

profile of v0, /device:TPU:25, one launch (start us, length us, event | category | flops | bytes accessed | tf_op | source)
XLA Modules:
  0.0 142.2 jit_solution(3390847744765210426)
XLA Ops:
  8.5 4.2 %prepare.1 = (bf16[256,512]{1,0:T(8,128)(2,1)S(1)}, bf16[256,512]{1,0:T(8,128)(2,1)S(1)}, bf16[256,256]{1,0:T(8,128)(2,1)S(1)}, bf16[256,256]{1,0:T(8,128)(2,1)S...) custom-call(s32[6]{0:T(128)S(1)} %stack.27.refs_0_.place, ...), custom_call_target="tpu_custom_call" | custom-call | tf_op jit(solution)/shard_map/prepare/pallas_call | solution.py:510
  13.8 2.3 %collective-permute-done.refs_0_ = bf16[64,256]{1,0:T(8,128)(2,1)S(1)} collective-permute-done((bf16[64,256]{1,0:T(8,128)(2,1)S(1)}, bf16[64,256]{1,0:T(8,128)(2,1)S(1)}, u32[]{:S(2)}, u32[]{:S(2)}) %collective-permute-start) | collective-permute-done | bytes 32800 | tf_op jit(solution)/shard_map/ppermute | solution.py:33
  16.7 3.0 %collective-permute-done.2.refs_2_ = bf16[64,256]{1,0:T(8,128)(2,1)S(1)} collective-permute-done((bf16[64,256]{1,0:T(8,128)(2,1)S(1)}, bf16[64,256]{1,0:T(8,128)(2,1)S(1)}, u32[]{:S(2)}, u32[]{:S(2)}) %collective-permute-start.2) | collective-permute-done | bytes 32800 | tf_op jit(solution)/shard_map/ppermute | solution.py:33
  20.3 1.4 collective-permute-start.3
  21.7 2.5 %collective-permute-done.3.refs_1_.refs_3_ = bf16[264,256]{1,0:T(8,128)(2,1)S(1)} collective-permute-done((bf16[264,256]{1,0:T(8,128)(2,1)S(1)}, bf16[264,256]{1,0:T(8,128)(2,1)S(1)}, u32[]{:S(2)}, u32[]{:S(2)}) %collective-permute-start.3) | collective-permute-done | bytes 135200 | tf_op jit(solution)/shard_map/ppermute | solution.py:33
  24.2 2.5 %collective-permute-start.5 = (bf16[264,256]{1,0:T(8,128)(2,1)S(1)}, bf16[264,256]{1,0:T(8,128)(2,1)S(1)}, u32[]{:S(2)}, u32[]{:S(2)}) collective-permute-start(bf16[264,256]{1,0:T(8,128)(2,1)S(1)} %get-tuple-element.39), channel_id=1, source_target_pairs={{0,24},{4,28},{8,16},{12,20},{16,8},{20,12},{24,0},{28,4},{1,25},{... | collective-permute-start | bytes 405512 | tf_op jit(solution)/shard_map/ppermute | solution.py:33
  31.5 4.5 %collective-permute-done.27.refs_1_.refs_8_ = bf16[256,512]{1,0:T(8,128)(2,1)S(1)} collective-permute-done((bf16[256,512]{1,0:T(8,128)(2,1)S(1)}, bf16[256,512]{1,0:T(8,128)(2,1)S(1)}, u32[]{:S(2)}, u32[]{:S(2)}) %collective-permute-start.27) | collective-permute-done | bytes 262176 | tf_op jit(solution)/shard_map/ppermute | solution.py:33
  35.9 11.2 %collective-permute-start.6 = (bf16[4,136,256]{2,1,0:T(8,128)(2,1)S(1)}, bf16[4,136,256]{2,1,0:T(8,128)(2,1)S(1)}, u32[]{:S(2)}, u32[]{:S(2)}) collective-permute-start(bf16[4,136,256]{2,1,0:T(8,128)(2,1)S(1)} %ssplit.1), channel_id=1, source_target_pairs={{0,4},{4,0},{8,12},{12,8},{16,20},{20,16},{24,28},{28,24},{1,5},{5... | collective-permute-start | bytes 835592 | tf_op jit(solution)/shard_map/ppermute | solution.py:33
  47.4 6.9 %collective-permute-done.29.refs_3_.refs_10_ = bf16[256,512]{1,0:T(8,128)(2,1)S(1)} collective-permute-done((bf16[256,512]{1,0:T(8,128)(2,1)S(1)}, bf16[256,512]{1,0:T(8,128)(2,1)S(1)}, u32[]{:S(2)}, u32[]{:S(2)}) %collective-permute-start.29) | collective-permute-done | bytes 262176 | tf_op jit(solution)/shard_map/ppermute | solution.py:33
  54.3 3.5 %collective-permute-start.10 = (bf16[128,2048]{1,0:T(8,128)(2,1)}, bf16[128,2048]{1,0:T(8,128)(2,1)S(1)}, u32[]{:S(2)}, u32[]{:S(2)}) collective-permute-start(bf16[128,2048]{1,0:T(8,128)(2,1)} %refs_5_.3), channel_id=1, source_target_pairs={{0,4},{4,0},{8,12},{12,8},{16,20},{20,16},{24,28},{28,24},{1,5},{5... | collective-permute-start | bytes 1572872 | tf_op jit(solution)/shard_map/ppermute | solution.py:33
  63.2 1.6 %collective-permute-start.13 = (bf16[128,2048]{1,0:T(8,128)(2,1)S(1)}, bf16[128,2048]{1,0:T(8,128)(2,1)S(1)}, u32[]{:S(2)}, u32[]{:S(2)}) collective-permute-start(bf16[128,2048]{1,0:T(8,128)(2,1)S(1)} %collective-permute-done.9.refs_3_.refs_8_), channel_id=1, source_target_pairs={{0,4},{4,0},{8,12},{12,8},{16,20},{20,16},{24,28},{28,24},{1,5},{5... | collective-permute-start | bytes 1572872 | tf_op jit(solution)/shard_map/ppermute | solution.py:33
  65.3 2.1 %collective-permute-done.17.refs_16_ = bf16[128,2048]{1,0:T(8,128)(2,1)S(1)} collective-permute-done((bf16[128,2048]{1,0:T(8,128)(2,1)S(1)}, bf16[128,2048]{1,0:T(8,128)(2,1)S(1)}, u32[]{:S(2)}, u32[]{:S(2)}) %collective-permute-start.17) | collective-permute-done | bytes 524320 | tf_op jit(solution)/shard_map/ppermute | solution.py:59
  67.4 1.3 collective-permute-start.21
  68.7 1.5 %collective-permute-start.25 = (bf16[16,2048]{1,0:T(8,128)(2,1)S(1)}, bf16[16,2048]{1,0:T(8,128)(2,1)S(1)}, u32[]{:S(2)}, u32[]{:S(2)}) collective-permute-start(bf16[16,2048]{1,0:T(8,128)(2,1)S(1)} %tail.1), channel_id=1, source_target_pairs={{12,28},{13,29},{14,30},{15,31}} | collective-permute-start | bytes 196616 | tf_op jit(solution)/shard_map/ppermute | solution.py:506
  71.6 3.4 %collective-permute-done.25 = bf16[16,2048]{1,0:T(8,128)(2,1)S(1)} collective-permute-done((bf16[16,2048]{1,0:T(8,128)(2,1)S(1)}, bf16[16,2048]{1,0:T(8,128)(2,1)S(1)}, u32[]{:S(2)}, u32[]{:S(2)}) %collective-permute-start.25) | collective-permute-done | bytes 65568 | tf_op jit(solution)/shard_map/ppermute | solution.py:506
  75.7 7.9 %state.1 = (bf16[2048,128]{1,0:T(8,128)(2,1)S(1)}, f32[16,8,128]{2,1,0:T(8,128)S(1)}, f32[16,8,128]{2,1,0:T(8,128)S(1)}, bf16[2064,2048]{1,0:T(8,128)(2,1)S(1)}) custom-call(s32[6]{0:T(128)S(1)} %stack.27.refs_0_.place, f32[8,128]{1,0:T(8,128)S(1)} %get-tuple-element.29.refs_1_, f32[8,128]{1,0:T(8,128)S(1)} %get-tuple-element.30.refs_2_, ...), custom_call_target="tpu_custom_call" | custom-call | tf_op jit(solution)/shard_map/state/pallas_call | solution.py:635
  84.3 3.5 %collective-permute-start.34 = (bf16[512,256]{1,0:T(8,128)(2,1)S(1)}, bf16[512,256]{1,0:T(8,128)(2,1)S(1)}, u32[]{:S(2)}, u32[]{:S(2)}) collective-permute-start(bf16[512,256]{1,0:T(8,128)(2,1)S(1)} %pad_maximum_fusion.1), channel_id=1, source_target_pairs={{0,24},{4,28},{8,16},{12,20},{16,8},{20,12},{24,0},{28,4},{1,25},{... | collective-permute-start | bytes 786440 | tf_op jit(solution)/shard_map/ppermute | solution.py:33
  87.9 12.9 %mixer.1 = (bf16[2048,256]{1,0:T(8,128)(2,1)S(1)}, f32[16,128,256]{2,1,0:T(8,128)S(1)}, bf16[128,256]{1,0:T(8,128)(2,1)S(1)}, f32[8,256]{1,0:T(8,128)}) custom-call(s32[6]{0:T(128)S(1)} %stack.27.refs_0_.place, f32[8,256]{1,0:T(8,128)S(1)} %get-tuple-element.41.refs_1_, bf16[2048,128]{1,0:T(8,128)(2,1)S(1)} %get-tuple-element.40.refs_2_.half, ...), custom_call_target="tpu_custom_call" | custom-call | tf_op jit(solution)/shard_map/mixer/pallas_call | solution.py:650
  102.1 2.3 %collective-permute-done.33.refs_3_ = bf16[512,256]{1,0:T(8,128)(2,1)S(1)} collective-permute-done((bf16[512,256]{1,0:T(8,128)(2,1)S(1)}, bf16[512,256]{1,0:T(8,128)(2,1)S(1)}, u32[]{:S(2)}, u32[]{:S(2)}) %collective-permute-start.33) | collective-permute-done | bytes 262176 | tf_op jit(solution)/shard_map/ppermute | solution.py:33
  104.3 4.5 %gate.1 = bf16[2048,256]{1,0:T(8,128)(2,1)S(1)} custom-call(s32[6]{0:T(128)S(1)} %stack.27.refs_0_.place, bf16[512,256]{1,0:T(8,128)(2,1)S(1)} %pad_maximum_fusion.refs_1_, bf16[512,256]{1,0:T(8,128)(2,1)S(1)} %collective-permute-done.32.refs_2_, bf16[512,256]{1,0:T(8,128)(2,1)S(1)} %collective-permute-done.33.refs_3_, ...), custom_call_target="tpu_custom_call" | custom-call | tf_op jit(solution)/shard_map/gate/pallas_call | solution.py:674
  108.9 3.9 %collective-permute-done.35.prior = bf16[128,256]{1,0:T(8,128)(2,1)S(1)} collective-permute-done((bf16[128,256]{1,0:T(8,128)(2,1)S(1)}, bf16[128,256]{1,0:T(8,128)(2,1)S(1)}, u32[]{:S(2)}, u32[]{:S(2)}) %collective-permute-start.35) | collective-permute-done | bytes 65568 | tf_op jit(solution)/shard_map/ppermute | solution.py:672
  112.8 6.6 %scan.1 = bf16[2048,256]{1,0:T(8,128)(2,1)S(1)} custom-call(s32[6]{0:T(128)S(1)} %stack.27.refs_0_.place, bf16[2048,128]{1,0:T(8,128)(2,1)S(1)} %get-tuple-element.40.refs_2_.half, bf16[2048,128]{1,0:T(8,128)(2,1)S(1)} %collective-permute-done.26.refs_3_.half_other, bf16[2048,256]{1,0:T(8,128)(2,1)S(1)} %get-tuple-element.47.x_vals, ...), custom_call_target="tpu_custom_call" | custom-call | tf_op jit(solution)/shard_map/scan/pallas_call | solution.py:684
  119.4 21.4 %all_to_all.9.refs_0_ = bf16[16,128,256]{2,1,0:T(8,128)(2,1)S(1)} all-to-all(bf16[16,128,256]{2,1,0:T(8,128)(2,1)S(1)} %bitcast.10), channel_id=1, replica_groups={{0,1,2,3,4,5,6,7,8,9,10,11,12,13,14,15},{16,17,18,19,20,21,22,23,24,25,..., dimensions={0} | all-to-all | bytes 2097152 | tf_op jit(solution)/shard_map/all_to_all | solution.py:694
  140.7 1.4 norm.1
  (87 shorter events, 25.7 us)
Async XLA Ops:
  0.0 27.8 %collective-permute-start.7 = (bf16[128,2048]{1,0:T(8,128)(2,1)}, bf16[128,2048]{1,0:T(8,128)(2,1)S(1)}, u32[]{:S(2)}, u32[]{:S(2)}) collective-permute-start(bf16[128,2048]{1,0:T(8,128)(2,1)} %refs_5_.3), channel_id=1, source_target_pairs={{0,1},{1,0},{2,3},{3,2},{4,5},{5,4},{6,7},{7,6},{8,9},{9,8},{10,11... | collective-permute-start | bytes 1572872 | tf_op jit(solution)/shard_map/ppermute | solution.py:33
  1.2 26.7 %collective-permute-start.14 = (bf16[128,2048]{1,0:T(8,128)(2,1)}, bf16[128,2048]{1,0:T(8,128)(2,1)S(1)}, u32[]{:S(2)}, u32[]{:S(2)}) collective-permute-start(bf16[128,2048]{1,0:T(8,128)(2,1)} %refs_5_.3), channel_id=1, source_target_pairs={{0,8},{4,12},{8,0},{12,4},{16,24},{20,28},{24,16},{28,20},{1,9},{5... | collective-permute-start | bytes 1572872 | tf_op jit(solution)/shard_map/ppermute | solution.py:33
  1.4 26.9 %collective-permute-start.8 = (bf16[128,2048]{1,0:T(8,128)(2,1)}, bf16[128,2048]{1,0:T(8,128)(2,1)S(1)}, u32[]{:S(2)}, u32[]{:S(2)}) collective-permute-start(bf16[128,2048]{1,0:T(8,128)(2,1)} %refs_5_.3), channel_id=1, source_target_pairs={{0,2},{1,3},{2,0},{3,1},{4,6},{5,7},{6,4},{7,5},{8,10},{9,11},{10,... | collective-permute-start | bytes 1572872 | tf_op jit(solution)/shard_map/ppermute | solution.py:33
  24.2 6.2 %collective-permute-start.5 = (bf16[264,256]{1,0:T(8,128)(2,1)S(1)}, bf16[264,256]{1,0:T(8,128)(2,1)S(1)}, u32[]{:S(2)}, u32[]{:S(2)}) collective-permute-start(bf16[264,256]{1,0:T(8,128)(2,1)S(1)} %get-tuple-element.39), channel_id=1, source_target_pairs={{0,24},{4,28},{8,16},{12,20},{16,8},{20,12},{24,0},{28,4},{1,25},{... | collective-permute-start | bytes 405512 | tf_op jit(solution)/shard_map/ppermute | solution.py:33
  27.8 8.1 %collective-permute-start.27 = (bf16[256,512]{1,0:T(8,128)(2,1)S(1)}, bf16[256,512]{1,0:T(8,128)(2,1)S(1)}, u32[]{:S(2)}, u32[]{:S(2)}) collective-permute-start(bf16[256,512]{1,0:T(8,128)(2,1)S(1)} %get-tuple-element.45), channel_id=1, source_target_pairs={{0,8},{4,12},{8,0},{12,4},{16,24},{20,28},{24,16},{28,20},{1,9},{5... | collective-permute-start | bytes 786440 | tf_op jit(solution)/shard_map/ppermute | solution.py:33
  27.8 19.3 %collective-permute-start.28 = (bf16[256,512]{1,0:T(8,128)(2,1)S(1)}, bf16[256,512]{1,0:T(8,128)(2,1)S(1)}, u32[]{:S(2)}, u32[]{:S(2)}) collective-permute-start(bf16[256,512]{1,0:T(8,128)(2,1)S(1)} %get-tuple-element.44.refs_0_.refs_7_), channel_id=1, source_target_pairs={{0,16},{4,20},{8,24},{12,28},{16,0},{20,4},{24,8},{28,12},{1,17},{... | collective-permute-start | bytes 786440 | tf_op jit(solution)/shard_map/ppermute | solution.py:33
  27.9 29.9 %collective-permute-start.15 = (bf16[128,2048]{1,0:T(8,128)(2,1)S(1)}, bf16[128,2048]{1,0:T(8,128)(2,1)S(1)}, u32[]{:S(2)}, u32[]{:S(2)}) collective-permute-start(bf16[128,2048]{1,0:T(8,128)(2,1)S(1)} %collective-permute-done.14.refs_13_), channel_id=1, source_target_pairs={{0,1},{1,0},{2,3},{3,2},{4,5},{5,4},{6,7},{7,6},{8,9},{9,8},{10,11... | collective-permute-start | bytes 1572872 | tf_op jit(solution)/shard_map/ppermute | solution.py:33
  28.3 30.0 %collective-permute-start.16 = (bf16[128,2048]{1,0:T(8,128)(2,1)S(1)}, bf16[128,2048]{1,0:T(8,128)(2,1)S(1)}, u32[]{:S(2)}, u32[]{:S(2)}) collective-permute-start(bf16[128,2048]{1,0:T(8,128)(2,1)S(1)} %collective-permute-done.14.refs_13_), channel_id=1, source_target_pairs={{0,2},{1,3},{2,0},{3,1},{4,6},{5,7},{6,4},{7,5},{8,10},{9,11},{10,... | collective-permute-start | bytes 1572872 | tf_op jit(solution)/shard_map/ppermute | solution.py:33
  30.5 28.5 %collective-permute-start.9 = (bf16[128,2048]{1,0:T(8,128)(2,1)S(1)}, bf16[128,2048]{1,0:T(8,128)(2,1)S(1)}, u32[]{:S(2)}, u32[]{:S(2)}) collective-permute-start(bf16[128,2048]{1,0:T(8,128)(2,1)S(1)} %either.2), channel_id=1, source_target_pairs={{0,2},{1,3},{2,0},{3,1},{4,5},{5,4},{6,7},{7,6},{8,10},{9,11},{10,... | collective-permute-start | bytes 1572872 | tf_op jit(solution)/shard_map/ppermute | solution.py:59
  35.9 21.8 %collective-permute-start.6 = (bf16[4,136,256]{2,1,0:T(8,128)(2,1)S(1)}, bf16[4,136,256]{2,1,0:T(8,128)(2,1)S(1)}, u32[]{:S(2)}, u32[]{:S(2)}) collective-permute-start(bf16[4,136,256]{2,1,0:T(8,128)(2,1)S(1)} %ssplit.1), channel_id=1, source_target_pairs={{0,4},{4,0},{8,12},{12,8},{16,20},{20,16},{24,28},{28,24},{1,5},{5... | collective-permute-start | bytes 835592 | tf_op jit(solution)/shard_map/ppermute | solution.py:33
  47.2 7.1 %collective-permute-start.29 = (bf16[256,512]{1,0:T(8,128)(2,1)S(1)}, bf16[256,512]{1,0:T(8,128)(2,1)S(1)}, u32[]{:S(2)}, u32[]{:S(2)}) collective-permute-start(bf16[256,512]{1,0:T(8,128)(2,1)S(1)} %get-tuple-element.45), channel_id=1, source_target_pairs={{0,24},{4,28},{8,16},{12,20},{16,8},{20,12},{24,0},{28,4},{1,25},{... | collective-permute-start | bytes 786440 | tf_op jit(solution)/shard_map/ppermute | solution.py:33
  54.3 6.9 %collective-permute-start.10 = (bf16[128,2048]{1,0:T(8,128)(2,1)}, bf16[128,2048]{1,0:T(8,128)(2,1)S(1)}, u32[]{:S(2)}, u32[]{:S(2)}) collective-permute-start(bf16[128,2048]{1,0:T(8,128)(2,1)} %refs_5_.3), channel_id=1, source_target_pairs={{0,4},{4,0},{8,12},{12,8},{16,20},{20,16},{24,28},{28,24},{1,5},{5... | collective-permute-start | bytes 1572872 | tf_op jit(solution)/shard_map/ppermute | solution.py:33
  59.0 8.4 %collective-permute-start.17 = (bf16[128,2048]{1,0:T(8,128)(2,1)S(1)}, bf16[128,2048]{1,0:T(8,128)(2,1)S(1)}, u32[]{:S(2)}, u32[]{:S(2)}) collective-permute-start(bf16[128,2048]{1,0:T(8,128)(2,1)S(1)} %either.3), channel_id=1, source_target_pairs={{0,2},{1,3},{2,0},{3,1},{4,5},{5,4},{6,7},{7,6},{8,10},{9,11},{10,... | collective-permute-start | bytes 1572872 | tf_op jit(solution)/shard_map/ppermute | solution.py:59
  63.2 12.3 %collective-permute-start.13 = (bf16[128,2048]{1,0:T(8,128)(2,1)S(1)}, bf16[128,2048]{1,0:T(8,128)(2,1)S(1)}, u32[]{:S(2)}, u32[]{:S(2)}) collective-permute-start(bf16[128,2048]{1,0:T(8,128)(2,1)S(1)} %collective-permute-done.9.refs_3_.refs_8_), channel_id=1, source_target_pairs={{0,4},{4,0},{8,12},{12,8},{16,20},{20,16},{24,28},{28,24},{1,5},{5... | collective-permute-start | bytes 1572872 | tf_op jit(solution)/shard_map/ppermute | solution.py:33
  64.8 10.8 %collective-permute-start.19 = (bf16[128,2048]{1,0:T(8,128)(2,1)S(1)}, bf16[128,2048]{1,0:T(8,128)(2,1)S(1)}, u32[]{:S(2)}, u32[]{:S(2)}) collective-permute-start(bf16[128,2048]{1,0:T(8,128)(2,1)S(1)} %collective-permute-done.15.first.refs_14_), channel_id=1, source_target_pairs={{0,4},{4,0},{8,12},{12,8},{16,20},{20,16},{24,28},{28,24},{1,5},{5... | collective-permute-start | bytes 1572872 | tf_op jit(solution)/shard_map/ppermute | solution.py:33
  64.9 10.8 %collective-permute-start.20 = (bf16[128,2048]{1,0:T(8,128)(2,1)S(1)}, bf16[128,2048]{1,0:T(8,128)(2,1)S(1)}, u32[]{:S(2)}, u32[]{:S(2)}) collective-permute-start(bf16[128,2048]{1,0:T(8,128)(2,1)S(1)} %collective-permute-done.16.second.refs_15_), channel_id=1, source_target_pairs={{0,4},{4,0},{8,12},{12,8},{16,20},{20,16},{24,28},{28,24},{1,5},{5... | collective-permute-start | bytes 1572872 | tf_op jit(solution)/shard_map/ppermute | solution.py:33
  67.4 8.2 %collective-permute-start.21 = (bf16[128,2048]{1,0:T(8,128)(2,1)S(1)}, bf16[128,2048]{1,0:T(8,128)(2,1)S(1)}, u32[]{:S(2)}, u32[]{:S(2)}) collective-permute-start(bf16[128,2048]{1,0:T(8,128)(2,1)S(1)} %collective-permute-done.17.refs_16_), channel_id=1, source_target_pairs={{0,4},{4,0},{8,12},{12,8},{16,20},{20,16},{24,28},{28,24},{1,5},{5... | collective-permute-start | bytes 1572872 | tf_op jit(solution)/shard_map/ppermute | solution.py:33
  68.7 6.3 %collective-permute-start.25 = (bf16[16,2048]{1,0:T(8,128)(2,1)S(1)}, bf16[16,2048]{1,0:T(8,128)(2,1)S(1)}, u32[]{:S(2)}, u32[]{:S(2)}) collective-permute-start(bf16[16,2048]{1,0:T(8,128)(2,1)S(1)} %tail.1), channel_id=1, source_target_pairs={{12,28},{13,29},{14,30},{15,31}} | collective-permute-start | bytes 196616 | tf_op jit(solution)/shard_map/ppermute | solution.py:506
  75.0 9.1 %collective-permute-start.31 = (bf16[256,512]{1,0:T(8,128)(2,1)S(1)}, bf16[256,512]{1,0:T(8,128)(2,1)S(1)}, u32[]{:S(2)}, u32[]{:S(2)}) collective-permute-start(bf16[256,512]{1,0:T(8,128)(2,1)S(1)} %get-tuple-element.49), channel_id=1, source_target_pairs={{0,4},{4,0},{8,12},{12,8},{16,20},{20,16},{24,28},{28,24},{1,5},{5... | collective-permute-start | bytes 786440 | tf_op jit(solution)/shard_map/ppermute | solution.py:33
  75.5 12.3 %collective-permute-start.30 = (bf16[4,256,256]{2,1,0:T(8,128)(2,1)S(1)}, bf16[4,256,256]{2,1,0:T(8,128)(2,1)S(1)}, u32[]{:S(2)}, u32[]{:S(2)}) collective-permute-start(bf16[4,256,256]{2,1,0:T(8,128)(2,1)S(1)} %xsplit.1), channel_id=1, source_target_pairs={{0,4},{4,0},{8,12},{12,8},{16,20},{20,16},{24,28},{28,24},{1,5},{5... | collective-permute-start | bytes 1572872 | tf_op jit(solution)/shard_map/ppermute | solution.py:33
  84.1 17.9 %collective-permute-start.32 = (bf16[512,256]{1,0:T(8,128)(2,1)S(1)}, bf16[512,256]{1,0:T(8,128)(2,1)S(1)}, u32[]{:S(2)}, u32[]{:S(2)}) collective-permute-start(bf16[512,256]{1,0:T(8,128)(2,1)S(1)} %pad_maximum_fusion.1), channel_id=1, source_target_pairs={{0,8},{4,12},{8,0},{12,4},{16,24},{20,28},{24,16},{28,20},{1,9},{5... | collective-permute-start | bytes 786440 | tf_op jit(solution)/shard_map/ppermute | solution.py:33
  84.3 20.1 %collective-permute-start.33 = (bf16[512,256]{1,0:T(8,128)(2,1)S(1)}, bf16[512,256]{1,0:T(8,128)(2,1)S(1)}, u32[]{:S(2)}, u32[]{:S(2)}) collective-permute-start(bf16[512,256]{1,0:T(8,128)(2,1)S(1)} %pad_maximum_fusion.refs_1_), channel_id=1, source_target_pairs={{0,16},{4,20},{8,24},{12,28},{16,0},{20,4},{24,8},{28,12},{1,17},{... | collective-permute-start | bytes 786440 | tf_op jit(solution)/shard_map/ppermute | solution.py:33
  84.3 20.0 %collective-permute-start.34 = (bf16[512,256]{1,0:T(8,128)(2,1)S(1)}, bf16[512,256]{1,0:T(8,128)(2,1)S(1)}, u32[]{:S(2)}, u32[]{:S(2)}) collective-permute-start(bf16[512,256]{1,0:T(8,128)(2,1)S(1)} %pad_maximum_fusion.1), channel_id=1, source_target_pairs={{0,24},{4,28},{8,16},{12,20},{16,8},{20,12},{24,0},{28,4},{1,25},{... | collective-permute-start | bytes 786440 | tf_op jit(solution)/shard_map/ppermute | solution.py:33
  100.8 12.0 %collective-permute-start.35 = (bf16[128,256]{1,0:T(8,128)(2,1)S(1)}, bf16[128,256]{1,0:T(8,128)(2,1)S(1)}, u32[]{:S(2)}, u32[]{:S(2)}) collective-permute-start(bf16[128,256]{1,0:T(8,128)(2,1)S(1)} %get-tuple-element.52), channel_id=1, source_target_pairs={{0,16},{4,20},{8,24},{12,28},{1,17},{5,21},{9,25},{13,29},{2,18},{... | collective-permute-start | bytes 196616 | tf_op jit(solution)/shard_map/ppermute | solution.py:672
  (21 other events, 172.1 us)
where the time goes:
time: 144 us; the launch traced here: 142 us
  Pallas kernels  42.5 us (30%)
  starting transfers between devices  38 us (26%)
  waiting for transfers between devices  33 us (23%)
  blocking collectives  21.4 us (15%)
  local copies, waits for them, and re-layouts  6.89 us (5%)
    ppermute x29, starting transfers between devices, swapped(): return lax.ppermute(x, axis, pairs)  32.4 us
    ppermute x29, waiting for transfers between devices, swapped(): return lax.ppermute(x, axis, pairs)  23.6 us
    all_to_all x1, blocking collectives, on_device(): lax.all_to_all(gated, ('ctx', 'inner'), 0, 0, axis_index_groups=teams, ti...  21.4 us
    pallas_call x1, Pallas kernels, on_device(): pl.pallas_call(lambda *refs: mixer_kernel(inner_count, shared, z_count, *...  12.9 us
    pallas_call x1, Pallas kernels, on_device(): pl.pallas_call(lambda *refs: state_kernel(inner_count, *refs), in_specs=[...  7.89 us
    unnamed x19, local copies, waits for them, and re-layouts  6.79 us
    pallas_call x1, Pallas kernels, on_device(): pl.pallas_call(scan_kernel, in_specs=[SMEM] + [VMEM] * 8, out_specs=VMEM,...  6.59 us
    pallas_call x1, Pallas kernels, on_device(): pl.pallas_call(lambda *refs: gate_kernel(inner_count, shared, z_count, *r...  4.53 us
  transfers between devices with their start and end apart: 36, of which 11 were waited for; matrix products, arithmetic and copies ran while one was open for 1% of the time, Pallas kernels for 24%

commit v1 on v0

--- a/solution.py
+++ b/solution.py
@@ -1,3 +1,5 @@
+import functools
+
 import jax
 import jax.numpy as jnp
 from jax import lax
@@ -21,19 +23,37 @@
 
 
 ANY = pl.BlockSpec(memory_space=pl.ANY)
+HBM = pl.BlockSpec(memory_space=pltpu.HBM)
 VMEM = pl.BlockSpec(memory_space=pltpu.VMEM)
-SMEM = pl.BlockSpec(memory_space=pltpu.SMEM)
 SMALL = pltpu.CompilerParams(vmem_limit_bytes=6 << 20)
 F32 = jnp.float32
 BF16 = jnp.bfloat16
 
 
+def group_of(inner_id, heads_over, members_over):
+    return inner_id * heads_over if heads_over else lax.div(inner_id, members_over)
+
+
+def here(heads_over, members_over):
+    ctx_id = lax.axis_index("ctx")
+    inner_id = lax.axis_index("inner")
+    z_id = lax.shift_right_logical(ctx_id, 1)
+    return (
+        ctx_id & (TEAM - 1),
+        inner_id,
+        z_id,
+        ctx_id & 1,
+        z_id & 1,
+        group_of(inner_id, heads_over, members_over),
+    )
+
+
 def swapped(x, axis, mask):
     pairs = [(i, i ^ mask) for i in range(lax.axis_size(axis))]
     return lax.ppermute(x, axis, pairs)
 
 
-def inner_blocks(block, place, inner_count, ctx_count):
+def inner_blocks(block, at, inner_count, ctx_count):
     if inner_count != 4:
         got = [block]
         step = 1
@@ -48,14 +68,14 @@
         for i in range(inner_count):
             pairs.append((c * inner_count + i, c * inner_count + (i ^ (1 if c % 2 else 2))))
     onward = pl.pallas_call(
-        either_kernel,
-        in_specs=[SMEM, ANY, ANY],
+        at(either_kernel),
+        in_specs=[ANY, ANY],
         out_specs=VMEM,
         out_shape=jax.ShapeDtypeStruct(block.shape, block.dtype),
         scratch_shapes=[pltpu.SemaphoreType.DMA],
         compiler_params=SMALL,
         name="either",
-    )(place, near_x, near_y)
+    )(near_x, near_y)
     far = lax.ppermute(onward, ("ctx", "inner"), pairs)
     return [block, near_x, near_y, far]
 
@@ -76,28 +96,43 @@
     return copies
 
 
-def prepare_kernel(heads_mine, place, project, state, step, taps, mixer_taps, step_bias, decay_log, *outs):
-    x_same, x_opposite, gate_same, gate_opposite, gate_sent, state_turned, step_same, step_opposite, taps_state = outs[:9]
-    taps_mixer, bias, rate = outs[9:]
+def side_columns(project, kind, index, size):
+    if size % LANES == 0:
+        return project[:, kind, pl.ds(pl.multiple_of(index * size, size), size)]
+    got = project[:, kind, :size]
+    for k in range(1, project.shape[2] // size):
+        got = jnp.where(index == k, project[:, kind, k * size : (k + 1) * size], got)
+    return got
+
+
+def mixer_columns_kernel(place, project, same, opposite, held, sems):
+    chunks = held.shape[0]
+    rows = held.shape[1]
+    pair = same.shape[1]
+    copies = [
+        pltpu.make_async_copy(project.at[pl.ds(c * rows, rows)], held.at[c], sems.at[c]) for c in range(chunks)
+    ]
+    for copy in copies:
+        copy.start()
+    for c, copy in enumerate(copies):
+        copy.wait()
+        same[c * rows : (c + 1) * rows] = side_columns(held.at[c], 1, place[4], pair)
+        opposite[c * rows : (c + 1) * rows] = side_columns(held.at[c], 1, 1 - place[4], pair)
+
+
+def prepare_kernel(heads_mine, place, *refs):
+    inputs, outs, held, sems = refs[:7], refs[7:17], refs[17:24], refs[24]
+    copies = [pltpu.make_async_copy(a, b, sems.at[i]) for i, (a, b) in enumerate(zip(inputs, held))]
+    for copy in copies:
+        copy.start()
+    project, state, step, taps, mixer_taps, step_bias, decay_log = held
+    for copy in copies[1:]:
+        copy.wait()
+    gate_same, gate_opposite, gate_sent, state_turned, step_same, step_opposite, taps_state = outs[:7]
+    taps_mixer, bias, rate = outs[7:]
     side, core = place[4], place[3]
-    pair = x_same.shape[1]
-    width = pair // 2
-
-    def columns(kind, index, size):
-        if size % LANES == 0:
-            return project[:, kind, pl.ds(pl.multiple_of(index * size, size), size)]
-        got = project[:, kind, :size]
-        for k in range(1, project.shape[2] // size):
-            got = jnp.where(index == k, project[:, kind, k * size : (k + 1) * size], got)
-        return got
-
-    other_side = 1 - side
-    x_same[...] = columns(1, side, pair)
-    x_opposite[...] = columns(1, other_side, pair)
-    gate_same[...] = columns(0, 2 * side + core, width)
-    gate_opposite[...] = columns(0, 2 * other_side + core, width)
-    gate_sent[:, :width] = columns(0, 2 * side + 1 - core, width)
-    gate_sent[:, width:] = columns(0, 2 * other_side + 1 - core, width)
+    width = gate_same.shape[1]
+
     cols = state.shape[2]
     target = lax.broadcasted_iota(jnp.int32, (2 * cols, cols), 0)
     source = lax.broadcasted_iota(jnp.int32, (2 * cols, cols), 1)
@@ -112,11 +147,9 @@
             preferred_element_type=F32,
         )
     state_turned[...] = turned.astype(BF16)
-    heads = step.shape[1]
-    rows = step.shape[0]
-    wide = jnp.concatenate([step[...].astype(F32), jnp.zeros((rows, LANES - heads), F32)], axis=1)
-    turned_step = wide.T[: 2 * PAD]
+    heads = step.shape[0]
     half = heads // 2
+    turned_step = jnp.concatenate([step[...].astype(F32), jnp.zeros((PAD, step.shape[1]), F32)], axis=0)
     low = turned_step[:PAD]
     high = turned_step[half : half + PAD]
     step_same[...] = jnp.where(side == 0, low, high).astype(BF16)
@@ -140,6 +173,12 @@
     for values, out in ((step_bias[...], bias), (-jnp.exp(decay_log[...]), rate)):
         picked = jnp.sum(jnp.where(own, values, 0.0), axis=1, keepdims=True)
         out[...] = jnp.broadcast_to(picked, out.shape)
+    copies[0].wait()
+    other_side = 1 - side
+    gate_same[...] = side_columns(project, 0, 2 * side + core, width)
+    gate_opposite[...] = side_columns(project, 0, 2 * other_side + core, width)
+    gate_sent[:, :width] = side_columns(project, 0, 2 * side + 1 - core, width)
+    gate_sent[:, width:] = side_columns(project, 0, 2 * other_side + 1 - core, width)
 
 
 def either_kernel(place, first, second, out, sem):
@@ -211,10 +250,11 @@
 
 def tail_kernel(place, *refs):
     blocks, out, sem = refs[:-2], refs[-2], refs[-1]
-    last = len(blocks) - 1
+    inner_count = len(blocks) // 2
     for d, block in enumerate(blocks):
-
-        @pl.when(place[1] == (last ^ d))
+        away, di = d // inner_count, d % inner_count
+
+        @pl.when(jnp.logical_and(place[3] == 1 - away, place[1] == (inner_count - 1) ^ di))
         def _():
             copy = pltpu.make_async_copy(block.at[pl.ds(block.shape[0] - HALO, HALO)], out, sem)
             copy.start()
@@ -459,13 +499,7 @@
 ):
     ctx_count = lax.axis_size("ctx")
     inner_count = lax.axis_size("inner")
-    ctx_id = lax.axis_index("ctx")
-    inner_id = lax.axis_index("inner")
-    core = ctx_id % 2
-    z_id = ctx_id // 2
     z_count = ctx_count // 2
-    side = z_id % 2
-    quarter = ctx_id % TEAM
     members = TEAM * inner_count
 
     rows_here, _, width_here = project_weight.shape
@@ -474,8 +508,11 @@
     heads_mine = heads_here // TEAM
     width_mine = width_here // TEAM
     per_group = H // G
-    group = inner_id * heads_here // per_group
-    place = jnp.stack([quarter, inner_id, z_id, core, side, group]).astype(jnp.int32)
+    spread_out = heads_here // per_group, per_group // heads_here
+
+    def at(kernel):
+        return lambda *refs: kernel(here(*spread_out), *refs)
+
     total = members * row_count
     count = total // SPAN
 
@@ -483,37 +520,54 @@
         return jax.ShapeDtypeStruct(shape, dtype)
 
     partner = swapped(tokens, "ctx", 2)
-    near = inner_blocks(tokens, place, inner_count, ctx_count)
-    beyond = inner_blocks(partner, place, inner_count, ctx_count)
-    blocks = (
-        near
-        + [swapped(b, "ctx", 1) for b in near]
-        + beyond
-        + [swapped(b, "ctx", 1) for b in beyond]
-    )
+    near = inner_blocks(tokens, at, inner_count, ctx_count)
+    beyond = inner_blocks(partner, at, inner_count, ctx_count)
+    blocks = near + [swapped(b, "ctx", 1) for b in near] + beyond + [swapped(b, "ctx", 1) for b in beyond]
     tail = pl.pallas_call(
-        tail_kernel,
-        in_specs=[SMEM] + [ANY] * len(near),
+        at(tail_kernel),
+        in_specs=[ANY] * (2 * inner_count),
         out_specs=VMEM,
         out_shape=sds((HALO, model_width), BF16),
         scratch_shapes=[pltpu.SemaphoreType.DMA],
         compiler_params=SMALL,
         name="tail",
-    )(place, *near)
+    )(*blocks[: 2 * inner_count])
     halo = jnp.zeros_like(tail)
-    for k in range(TEAM):
-        pairs = [(c - 1, c + k) for c in range(TEAM, ctx_count, TEAM)]
+    for k in range(2):
+        pairs = [
+            (c - 2 + m, c + 2 * k + m) for c in range(TEAM, ctx_count, TEAM) for m in range(2)
+        ]
         halo = halo + lax.ppermute(tail, "ctx", pairs)
 
     pair = 2 * width_mine
     slice_cols = state_weight.shape[2]
+    chunks = 4
+    x_sides = pl.pallas_call(
+        at(mixer_columns_kernel),
+        in_specs=[HBM],
+        out_specs=[VMEM] * 2,
+        out_shape=[sds((rows_here, pair), BF16)] * 2,
+        scratch_shapes=[
+            pltpu.VMEM((chunks, rows_here // chunks, 2, width_here), BF16),
+            pltpu.SemaphoreType.DMA((chunks,)),
+        ],
+        compiler_params=SMALL,
+        name="columns",
+    )(project_weight)
+    to_prepare = (
+        project_weight,
+        state_weight,
+        step_weight.T,
+        state_taps,
+        mixer_taps,
+        step_bias.reshape(1, -1),
+        decay_log.reshape(1, -1),
+    )
     prepared = pl.pallas_call(
-        lambda *refs: prepare_kernel(heads_mine, *refs),
-        in_specs=[SMEM] + [VMEM] * 7,
-        out_specs=[VMEM] * 12,
+        at(functools.partial(prepare_kernel, heads_mine)),
+        in_specs=[HBM] * 7,
+        out_specs=[VMEM] * 10,
         out_shape=[
-            sds((rows_here, pair), BF16),
-            sds((rows_here, pair), BF16),
             sds((rows_here, width_mine), BF16),
             sds((rows_here, width_mine), BF16),
             sds((rows_here, pair), BF16),
@@ -525,20 +579,12 @@
             sds((PAD, SPAN), F32),
             sds((PAD, SPAN), F32),
         ],
+        scratch_shapes=[pltpu.VMEM(v.shape, v.dtype) for v in to_prepare] + [pltpu.SemaphoreType.DMA((7,))],
         compiler_params=SMALL,
         name="prepare",
-    )(
-        place,
-        project_weight,
-        state_weight,
-        step_weight,
-        state_taps,
-        mixer_taps,
-        step_bias.reshape(1, -1),
-        decay_log.reshape(1, -1),
-    )
-    x_sides, gate_mine, gate_sent = prepared[0:2], prepared[2:4], prepared[4]
-    state_turned, step_sides = prepared[5], prepared[6:8]
+    )(*to_prepare)
+    gate_mine, gate_sent = prepared[0:2], prepared[2]
+    state_turned, step_sides = prepared[3], prepared[4:6]
 
     x_pieces = gathered_rows(lambda d: x_sides[d % 2], z_count)
 
@@ -546,36 +592,37 @@
         return lax.dynamic_slice_in_dim(piece, which * width_mine, width_mine, 1)
 
     x_sent = pl.pallas_call(
-        partner_columns_kernel,
-        in_specs=[SMEM] + [VMEM] * z_count,
+        at(partner_columns_kernel),
+        in_specs=[VMEM] * z_count,
         out_specs=VMEM,
         out_shape=sds((z_count, rows_here, width_mine), BF16),
         compiler_params=SMALL,
         name="xsplit",
-    )(place, *x_pieces)
+    )(*x_pieces)
     x_other = swapped(x_sent, "ctx", 1)
     if width_mine % LANES:
-        x_pieces = [of_core(p, core) for p in x_pieces]
+        x_pieces = [of_core(p, lax.axis_index("ctx") % 2) for p in x_pieces]
 
     part_rows = 2 * slice_cols // G
     if part_rows % (2 * HALO) == 0:
         sent = pl.pallas_call(
-            lambda *refs: sent_kernel(lambda j: j * heads_here // per_group, *refs),
-            in_specs=[SMEM, VMEM],
+            at(functools.partial(sent_kernel, lambda j: group_of(j, *spread_out))),
+            in_specs=[VMEM],
             out_specs=[VMEM] * (inner_count - 1),
             out_shape=[sds((part_rows, rows_here), BF16)] * (inner_count - 1),
             compiler_params=SMALL,
             name="sent",
-        )(place, state_turned)
+        )(state_turned)
         received = [swapped(sent[d - 1], "inner", d) for d in range(1, inner_count)]
-        payloads = pl.pallas_call(
-            payload_kernel,
-            in_specs=[SMEM] + [VMEM] * (inner_count + 2),
+        payload_call = pl.pallas_call(
+            at(payload_kernel),
+            in_specs=[VMEM] * (inner_count + 2),
             out_specs=[VMEM] * 2,
             out_shape=[sds((2 * N + PAD, rows_here), BF16)] * 2,
             compiler_params=SMALL,
             name="payload",
-        )(place, state_turned, *received, *step_sides)
+        )
+        payloads = payload_call(state_turned, *received, *step_sides)
     else:
         to_each = jnp.concatenate(
             [
@@ -590,22 +637,22 @@
         payloads = [jnp.concatenate([state_rows, s], axis=0) for s in step_sides]
     state_pieces = gathered_rows(lambda d: payloads[d % 2], z_count)
     state_sent = pl.pallas_call(
-        partner_rows_kernel,
-        in_specs=[SMEM] + [VMEM] * z_count,
+        at(partner_rows_kernel),
+        in_specs=[VMEM] * z_count,
         out_specs=VMEM,
         out_shape=sds((z_count, N + PAD, rows_here), BF16),
         compiler_params=SMALL,
         name="ssplit",
-    )(place, *state_pieces)
+    )(*state_pieces)
     state_other = swapped(state_sent, "ctx", 1)
     state_matrix = pl.pallas_call(
-        lambda *refs: assemble_kernel(heads_mine, *refs),
-        in_specs=[SMEM] + [VMEM] * (1 + z_count),
+        at(functools.partial(assemble_kernel, heads_mine)),
+        in_specs=[VMEM] * (1 + z_count),
         out_specs=VMEM,
         out_shape=sds((model_width, N + LANES), BF16),
         compiler_params=SMALL,
         name="assemble",
-    )(place, state_other, *state_pieces)
+    )(state_other, *state_pieces)
 
     gate_other = swapped(gate_sent, "ctx", 1)
     gate_chip = [
@@ -614,7 +661,7 @@
     ]
     gate_pieces = gathered_rows(lambda d: gate_chip[d % 2], z_count)
 
-    taps_state, taps_mine, bias_mine, rate_mine = prepared[8:]
+    taps_state, taps_mine, bias_mine, rate_mine = prepared[6:]
 
     shared = total * model_width <= 2**23
     tok_shape = (HALO + total, model_width)
@@ -633,14 +680,14 @@
     any_of = lambda values: [ANY] * len(values)
     state_outs = [sds((total, N), BF16), sds((count, PAD, SPAN), F32), sds((count, PAD, SPAN), F32)]
     outs = pl.pallas_call(
-        lambda *refs: state_kernel(inner_count, *refs),
-        in_specs=[SMEM, VMEM, VMEM, VMEM, VMEM] + any_of(source),
+        at(functools.partial(state_kernel, inner_count)),
+        in_specs=[VMEM] * 4 + any_of(source),
         out_specs=[VMEM] * (4 if shared else 3),
         out_shape=state_outs + ([sds(tok_shape, BF16)] if shared else []),
         scratch_shapes=scratch(0, N, not shared)[:-1],
         compiler_params=limit,
         name="state",
-    )(place, taps_state, bias_mine, rate_mine, state_matrix, *source)
+    )(taps_state, bias_mine, rate_mine, state_matrix, *source)
     half, step, cum = outs[:3]
     if shared:
         source = [outs[3]]
@@ -648,8 +695,8 @@
     half_other = swapped(half, "ctx", 1)
 
     x_vals, states, last_state, through = pl.pallas_call(
-        lambda *refs: mixer_kernel(inner_count, shared, z_count, *refs),
-        in_specs=[SMEM, VMEM, VMEM, VMEM, VMEM, VMEM, ANY] + any_of(x_pieces) + held_spec,
+        at(functools.partial(mixer_kernel, inner_count, shared, z_count)),
+        in_specs=[VMEM] * 5 + [ANY] + any_of(x_pieces) + held_spec,
         out_specs=[VMEM, VMEM, VMEM, VMEM],
         out_shape=[
             sds((total, width_mine), BF16),
@@ -660,7 +707,7 @@
         scratch_shapes=scratch(width_mine, width_mine, not shared),
         compiler_params=limit,
         name="mixer",
-    )(place, taps_mine, half, half_other, step, cum, x_other, *x_pieces, *source)
+    )(taps_mine, half, half_other, step, cum, x_other, *x_pieces, *source)
 
     hops = ctx_count // TEAM - 1
     pairs = [(c, c + TEAM) for c in range(ctx_count - TEAM)]
@@ -672,23 +719,23 @@
         prior = lax.ppermute(sent, "ctx", pairs)
 
     gate_values = pl.pallas_call(
-        lambda *refs: gate_kernel(inner_count, shared, z_count, *refs),
-        in_specs=[SMEM] + any_of(gate_pieces) + held_spec,
+        at(functools.partial(gate_kernel, inner_count, shared, z_count)),
+        in_specs=any_of(gate_pieces) + held_spec,
         out_specs=VMEM,
         out_shape=sds((total, width_mine), BF16),
         scratch_shapes=scratch(width_mine, 0, not shared),
         compiler_params=limit,
         name="gate",
-    )(place, *gate_pieces, *source)
+    )(*gate_pieces, *source)
 
     gated = pl.pallas_call(
-        scan_kernel,
-        in_specs=[SMEM] + [VMEM] * 8,
+        at(scan_kernel),
+        in_specs=[VMEM] * 8,
         out_specs=VMEM,
         out_shape=sds((total, width_mine), BF16),
         compiler_params=limit,
         name="scan",
-    )(place, half, half_other, x_vals, gate_values, step, cum, states, prior)
+    )(half, half_other, x_vals, gate_values, step, cum, states, prior)
 
     teams = [[t * members + m for m in range(members)] for t in range(ctx_count // TEAM)]
     parts = lax.all_to_all(
@@ -717,6 +764,4 @@
         P(),
     )
 
-    return jax.shard_map(
-        on_device, mesh=mesh, in_specs=placed, out_specs=P(("ctx", "inner"), None), check_vma=False
-    )
+    return jax.shard_map(on_device, mesh=mesh, in_specs=placed, out_specs=P(("ctx", "inner"), None), check_vma=False)

time: 144 us -> 160 us (1.11)
  starting transfers between devices: 38 us -> 49.1 us
  waiting for transfers between devices: 33 us -> 43.2 us
  Pallas kernels: 42.5 us -> 35 us
    ppermute x29, starting transfers between devices: 32.4 us -> 44.8 us  [swapped(): return lax.ppermute(x, axis, pairs)]
    pallas_call x13 -> x14, Pallas kernels: 41.1 us -> 33.6 us  [the longest x1 12.3 us: on_device(): pl.pallas_call(at(functools.partial(mixer_kernel, inner_count, shared, z_...]
    ppermute x29, waiting for transfers between devices: 23.6 us -> 30.7 us  [swapped(): return lax.ppermute(x, axis, pairs)]
    ppermute x4 -> x2, waiting for transfers between devices: 3.37 us -> 4.98 us  [on_device(): halo = halo + lax.ppermute(tail, 'ctx', pairs)]
    ppermute x4 -> x2, starting transfers between devices: 3.46 us -> 2.14 us  [on_device(): halo = halo + lax.ppermute(tail, 'ctx', pairs)]
    unnamed x19 -> x22, local copies, waits for them, and re-layouts: 6.79 us -> 7.89 us
  transfers between devices with their start and end apart: 36 -> 34, of which waited for: 11 -> 10; matrix products, arithmetic and copies ran while one was open for 1% -> 0% of each run, Pallas kernels for 24% -> 17%
where the time goes in v1:
time: 160 us; the launch traced here: 158 us
  starting transfers between devices  49.1 us (31%)
  waiting for transfers between devices  43.2 us (27%)
  Pallas kernels  35 us (22%)
  blocking collectives  22.1 us (14%)
  local copies, waits for them, and re-layouts  7.91 us (5%)
    ppermute x29, starting transfers between devices, swapped(): return lax.ppermute(x, axis, pairs)  44.8 us
    ppermute x29, waiting for transfers between devices, swapped(): return lax.ppermute(x, axis, pairs)  30.7 us
    all_to_all x1, blocking collectives, on_device(): lax.all_to_all(gated, ('ctx', 'inner'), 0, 0, axis_index_groups=teams, ti...  22.1 us
    pallas_call x1, Pallas kernels, on_device(): pl.pallas_call(at(functools.partial(mixer_kernel, inner_count, shared, z_...  12.3 us
    unnamed x22, local copies, waits for them, and re-layouts  7.89 us
    pallas_call x1, Pallas kernels, on_device(): pl.pallas_call(at(functools.partial(state_kernel, inner_count)), in_specs...  7.34 us
    pallas_call x1, Pallas kernels, on_device(): pl.pallas_call(at(scan_kernel), in_specs=[VMEM] * 8, out_specs=VMEM, out_...  6.03 us
    ppermute x2, waiting for transfers between devices, on_device(): halo = halo + lax.ppermute(tail, 'ctx', pairs)  4.98 us
  transfers between devices with their start and end apart: 34, of which 10 were waited for; matrix products, arithmetic and copies ran while one was open for 0% of the time, Pallas kernels for 17%

profile of v1, /device:TPU:25, one launch (start us, length us, event | category | flops | bytes accessed | tf_op | source)
XLA Modules:
  0.0 157.6 jit_solution(11362235913780592267)
XLA Ops:
  2.6 10.4 %collective-permute-done.14.refs_12_ = bf16[128,2048]{1,0:T(8,128)(2,1)S(1)} collective-permute-done((bf16[128,2048]{1,0:T(8,128)(2,1)}, bf16[128,2048]{1,0:T(8,128)(2,1)S(1)}, u32[]{:S(2)}, u32[]{:S(2)}) %collective-permute-start.14) | collective-permute-done | bytes 524320 | tf_op jit(solution)/shard_map/ppermute | solution.py:53
  21.1 2.1 %prepare.1 = (bf16[256,256]{1,0:T(8,128)(2,1)S(1)}, bf16[256,256]{1,0:T(8,128)(2,1)S(1)}, bf16[256,512]{1,0:T(8,128)(2,1)S(1)}, bf16[256,256]{1,0:T(8,128)(2,1)S...) custom-call(bf16[256,2,1024]{2,1,0:T(2,128)(2,1)S(1)} %copy-done, ...), custom_call_target="tpu_custom_call" | custom-call | tf_op jit(solution)/shard_map/prepare/pallas_call | solution.py:566
  23.5 3.2 %collective-permute-done.refs_1_ = bf16[64,256]{1,0:T(8,128)(2,1)S(1)} collective-permute-done((bf16[64,256]{1,0:T(8,128)(2,1)S(1)}, bf16[64,256]{1,0:T(8,128)(2,1)S(1)}, u32[]{:S(2)}, u32[]{:S(2)}) %collective-permute-start) | collective-permute-done | bytes 32800 | tf_op jit(solution)/shard_map/ppermute | solution.py:53
  26.9 2.5 %collective-permute-done.1.refs_2_ = bf16[64,256]{1,0:T(8,128)(2,1)S(1)} collective-permute-done((bf16[64,256]{1,0:T(8,128)(2,1)S(1)}, bf16[64,256]{1,0:T(8,128)(2,1)S(1)}, u32[]{:S(2)}, u32[]{:S(2)}) %collective-permute-start.1) | collective-permute-done | bytes 32800 | tf_op jit(solution)/shard_map/ppermute | solution.py:53
  30.6 2.5 %collective-permute-done.2.refs_3_ = bf16[64,256]{1,0:T(8,128)(2,1)S(1)} collective-permute-done((bf16[64,256]{1,0:T(8,128)(2,1)S(1)}, bf16[64,256]{1,0:T(8,128)(2,1)S(1)}, u32[]{:S(2)}, u32[]{:S(2)}) %collective-permute-start.2) | collective-permute-done | bytes 32800 | tf_op jit(solution)/shard_map/ppermute | solution.py:53
  33.8 5.5 %collective-permute-done.4.refs_2_.refs_3_ = bf16[264,256]{1,0:T(8,128)(2,1)S(1)} collective-permute-done((bf16[264,256]{1,0:T(8,128)(2,1)S(1)}, bf16[264,256]{1,0:T(8,128)(2,1)S(1)}, u32[]{:S(2)}, u32[]{:S(2)}) %collective-permute-start.4) | collective-permute-done | bytes 135200 | tf_op jit(solution)/shard_map/ppermute | solution.py:53
  42.0 3.8 %collective-permute-done.5.refs_3_.refs_4_ = bf16[264,256]{1,0:T(8,128)(2,1)S(1)} collective-permute-done((bf16[264,256]{1,0:T(8,128)(2,1)S(1)}, bf16[264,256]{1,0:T(8,128)(2,1)S(1)}, u32[]{:S(2)}, u32[]{:S(2)}) %collective-permute-start.5) | collective-permute-done | bytes 135200 | tf_op jit(solution)/shard_map/ppermute | solution.py:53
  45.8 2.1 %collective-permute-start.25 = (bf16[256,512]{1,0:T(8,128)(2,1)S(1)}, bf16[256,512]{1,0:T(8,128)(2,1)S(1)}, u32[]{:S(2)}, u32[]{:S(2)}) collective-permute-start(bf16[256,512]{1,0:T(8,128)(2,1)S(1)} %get-tuple-element.45), channel_id=1, source_target_pairs={{0,8},{4,12},{8,0},{12,4},{16,24},{20,28},{24,16},{28,20},{1,9},{5... | collective-permute-start | bytes 786440 | tf_op jit(solution)/shard_map/ppermute | solution.py:53
  47.9 3.1 %collective-permute-start.27 = (bf16[256,512]{1,0:T(8,128)(2,1)S(1)}, bf16[256,512]{1,0:T(8,128)(2,1)S(1)}, u32[]{:S(2)}, u32[]{:S(2)}) collective-permute-start(bf16[256,512]{1,0:T(8,128)(2,1)S(1)} %get-tuple-element.45), channel_id=1, source_target_pairs={{0,24},{4,28},{8,16},{12,20},{16,8},{20,12},{24,0},{28,4},{1,25},{... | collective-permute-start | bytes 786440 | tf_op jit(solution)/shard_map/ppermute | solution.py:53
  51.0 14.4 %collective-permute-start.10 = (bf16[128,2048]{1,0:T(8,128)(2,1)}, bf16[128,2048]{1,0:T(8,128)(2,1)S(1)}, u32[]{:S(2)}, u32[]{:S(2)}) collective-permute-start(bf16[128,2048]{1,0:T(8,128)(2,1)} %refs_4_.3), channel_id=1, source_target_pairs={{0,4},{4,0},{8,12},{12,8},{16,20},{20,16},{24,28},{28,24},{1,5},{5... | collective-permute-start | bytes 1572872 | tf_op jit(solution)/shard_map/ppermute | solution.py:53
  65.5 1.6 %collective-permute-start.11 = (bf16[128,2048]{1,0:T(8,128)(2,1)S(1)}, bf16[128,2048]{1,0:T(8,128)(2,1)S(1)}, u32[]{:S(2)}, u32[]{:S(2)}) collective-permute-start(bf16[128,2048]{1,0:T(8,128)(2,1)S(1)} %collective-permute-done.7.refs_0_.refs_1_.refs_5_), channel_id=1, source_target_pairs={{0,4},{4,0},{8,12},{12,8},{16,20},{20,16},{24,28},{28,24},{1,5},{5... | collective-permute-start | bytes 1572872 | tf_op jit(solution)/shard_map/ppermute | solution.py:53
  67.1 1.7 %collective-permute-start.12 = (bf16[128,2048]{1,0:T(8,128)(2,1)S(1)}, bf16[128,2048]{1,0:T(8,128)(2,1)S(1)}, u32[]{:S(2)}, u32[]{:S(2)}) collective-permute-start(bf16[128,2048]{1,0:T(8,128)(2,1)S(1)} %collective-permute-done.8.refs_1_.refs_2_.refs_6_), channel_id=1, source_target_pairs={{0,4},{4,0},{8,12},{12,8},{16,20},{20,16},{24,28},{28,24},{1,5},{5... | collective-permute-start | bytes 1572872 | tf_op jit(solution)/shard_map/ppermute | solution.py:53
  69.3 4.2 %collective-permute-start.6 = (bf16[4,136,256]{2,1,0:T(8,128)(2,1)S(1)}, bf16[4,136,256]{2,1,0:T(8,128)(2,1)S(1)}, u32[]{:S(2)}, u32[]{:S(2)}) collective-permute-start(bf16[4,136,256]{2,1,0:T(8,128)(2,1)S(1)} %ssplit.1), channel_id=1, source_target_pairs={{0,4},{4,0},{8,12},{12,8},{16,20},{20,16},{24,28},{28,24},{1,5},{5... | collective-permute-start | bytes 835592 | tf_op jit(solution)/shard_map/ppermute | solution.py:53
  74.2 3.0 %collective-permute-done.17.refs_15_ = bf16[128,2048]{1,0:T(8,128)(2,1)S(1)} collective-permute-done((bf16[128,2048]{1,0:T(8,128)(2,1)S(1)}, bf16[128,2048]{1,0:T(8,128)(2,1)S(1)}, u32[]{:S(2)}, u32[]{:S(2)}) %collective-permute-start.17) | collective-permute-done | bytes 524320 | tf_op jit(solution)/shard_map/ppermute | solution.py:79
  77.1 4.7 %collective-permute-start.21 = (bf16[128,2048]{1,0:T(8,128)(2,1)S(1)}, bf16[128,2048]{1,0:T(8,128)(2,1)S(1)}, u32[]{:S(2)}, u32[]{:S(2)}) collective-permute-start(bf16[128,2048]{1,0:T(8,128)(2,1)S(1)} %collective-permute-done.17.refs_15_), channel_id=1, source_target_pairs={{0,4},{4,0},{8,12},{12,8},{16,20},{20,16},{24,28},{28,24},{1,5},{5... | collective-permute-start | bytes 1572872 | tf_op jit(solution)/shard_map/ppermute | solution.py:53
  85.1 5.0 %collective-permute-done.23 = bf16[16,2048]{1,0:T(8,128)(2,1)S(1)} collective-permute-done((bf16[16,2048]{1,0:T(8,128)(2,1)S(1)}, bf16[16,2048]{1,0:T(8,128)(2,1)S(1)}, u32[]{:S(2)}, u32[]{:S(2)}) %collective-permute-start.23) | collective-permute-done | bytes 65568 | tf_op jit(solution)/shard_map/ppermute | solution.py:540
  91.5 7.3 %state.1 = (bf16[2048,128]{1,0:T(8,128)(2,1)S(1)}, f32[16,8,128]{2,1,0:T(8,128)S(1)}, f32[16,8,128]{2,1,0:T(8,128)S(1)}, bf16[2064,2048]{1,0:T(8,128)(2,1)S(1)}) custom-call(f32[8,128]{1,0:T(8,128)S(1)} %get-tuple-element.29.refs_0_, f32[8,128]{1,0:T(8,128)S(1)} %get-tuple-element.30.refs_1_, f32[8,128]{1,0:T(8,128)S(1)} %get-tuple-element.31.refs_2_, ...), custom_call_target="tpu_custom_call" | custom-call | tf_op jit(solution)/shard_map/state/pallas_call | solution.py:682
  99.6 3.5 %collective-permute-start.32 = (bf16[512,256]{1,0:T(8,128)(2,1)S(1)}, bf16[512,256]{1,0:T(8,128)(2,1)S(1)}, u32[]{:S(2)}, u32[]{:S(2)}) collective-permute-start(bf16[512,256]{1,0:T(8,128)(2,1)S(1)} %pad_maximum_fusion.1), channel_id=1, source_target_pairs={{0,24},{4,28},{8,16},{12,20},{16,8},{20,12},{24,0},{28,4},{1,25},{... | collective-permute-start | bytes 786440 | tf_op jit(solution)/shard_map/ppermute | solution.py:53
  103.1 12.3 %mixer.1 = (bf16[2048,256]{1,0:T(8,128)(2,1)S(1)}, f32[16,128,256]{2,1,0:T(8,128)S(1)}, bf16[128,256]{1,0:T(8,128)(2,1)S(1)}, f32[8,256]{1,0:T(8,128)}) custom-call(f32[8,256]{1,0:T(8,128)S(1)} %get-tuple-element.41.refs_0_, bf16[2048,128]{1,0:T(8,128)(2,1)S(1)} %get-tuple-element.40.refs_1_.refs_0_, ...), custom_call_target="tpu_custom_call" | custom-call | tf_op jit(solution)/shard_map/mixer/pallas_call | solution.py:697
  116.8 2.8 %collective-permute-done.31.refs_2_ = bf16[512,256]{1,0:T(8,128)(2,1)S(1)} collective-permute-done((bf16[512,256]{1,0:T(8,128)(2,1)S(1)}, bf16[512,256]{1,0:T(8,128)(2,1)S(1)}, u32[]{:S(2)}, u32[]{:S(2)}) %collective-permute-start.31) | collective-permute-done | bytes 262176 | tf_op jit(solution)/shard_map/ppermute | solution.py:53
  119.6 3.9 %gate.1.refs_3_ = bf16[2048,256]{1,0:T(8,128)(2,1)S(1)} custom-call(bf16[512,256]{1,0:T(8,128)(2,1)S(1)} %pad_maximum_fusion.refs_0_, bf16[512,256]{1,0:T(8,128)(2,1)S(1)} %collective-permute-done.30.refs_1_, bf16[512,256]{1,0:T(8,128)(2,1)S(1)} %collective-permute-done.31.refs_2_, bf16[512,256]{1,0:T(8,128)(2,1)S(1)} %collective-permute-done.32.refs_3_, ...), custom_call_target="tpu_custom_call" | custom-call | tf_op jit(solution)/shard_map/gate/pallas_call | solution.py:721
  123.6 4.5 %collective-permute-done.33.refs_7_ = bf16[128,256]{1,0:T(8,128)(2,1)S(1)} collective-permute-done((bf16[128,256]{1,0:T(8,128)(2,1)S(1)}, bf16[128,256]{1,0:T(8,128)(2,1)S(1)}, u32[]{:S(2)}, u32[]{:S(2)}) %collective-permute-start.33) | collective-permute-done | bytes 65568 | tf_op jit(solution)/shard_map/ppermute | solution.py:719
  128.0 6.0 %scan.1 = bf16[2048,256]{1,0:T(8,128)(2,1)S(1)} custom-call(bf16[2048,128]{1,0:T(8,128)(2,1)S(1)} %get-tuple-element.40.refs_1_.refs_0_, bf16[2048,128]{1,0:T(8,128)(2,1)S(1)} %collective-permute-done.24.refs_2_.refs_1_, bf16[2048,256]{1,0:T(8,128)(2,1)S(1)} %get-tuple-element.47.refs_2_, bf16[2048,256]{1,0:T(8,128)(2,1)S(1)} %gate.1.refs_3_, ...), custom_call_target="tpu_custom_call" | custom-call | tf_op jit(solution)/shard_map/scan/pallas_call | solution.py:731
  134.1 22.1 %all_to_all.9.refs_0_ = bf16[16,128,256]{2,1,0:T(8,128)(2,1)S(1)} all-to-all(bf16[16,128,256]{2,1,0:T(8,128)(2,1)S(1)} %bitcast.5), channel_id=1, replica_groups={{0,1,2,3,4,5,6,7,8,9,10,11,12,13,14,15},{16,17,18,19,20,21,22,23,24,25,..., dimensions={0} | all-to-all | bytes 2097152 | tf_op jit(solution)/shard_map/all_to_all | solution.py:741
  (86 shorter events, 25.1 us)
Async XLA Ops:
  0.0 13.0 %collective-permute-start.14 = (bf16[128,2048]{1,0:T(8,128)(2,1)}, bf16[128,2048]{1,0:T(8,128)(2,1)S(1)}, u32[]{:S(2)}, u32[]{:S(2)}) collective-permute-start(bf16[128,2048]{1,0:T(8,128)(2,1)} %refs_4_.3), channel_id=1, source_target_pairs={{0,8},{4,12},{8,0},{12,4},{16,24},{20,28},{24,16},{28,20},{1,9},{5... | collective-permute-start | bytes 1572872 | tf_op jit(solution)/shard_map/ppermute | solution.py:53
  0.2 33.1 %collective-permute-start.7 = (bf16[128,2048]{1,0:T(8,128)(2,1)}, bf16[128,2048]{1,0:T(8,128)(2,1)S(1)}, u32[]{:S(2)}, u32[]{:S(2)}) collective-permute-start(bf16[128,2048]{1,0:T(8,128)(2,1)} %refs_4_.3), channel_id=1, source_target_pairs={{0,1},{1,0},{2,3},{3,2},{4,5},{5,4},{6,7},{7,6},{8,9},{9,8},{10,11... | collective-permute-start | bytes 1572872 | tf_op jit(solution)/shard_map/ppermute | solution.py:53
  1.4 31.9 %collective-permute-start.8 = (bf16[128,2048]{1,0:T(8,128)(2,1)}, bf16[128,2048]{1,0:T(8,128)(2,1)S(1)}, u32[]{:S(2)}, u32[]{:S(2)}) collective-permute-start(bf16[128,2048]{1,0:T(8,128)(2,1)} %refs_4_.3), channel_id=1, source_target_pairs={{0,2},{1,3},{2,0},{3,1},{4,6},{5,7},{6,4},{7,5},{8,10},{9,11},{10,... | collective-permute-start | bytes 1572872 | tf_op jit(solution)/shard_map/ppermute | solution.py:53
  13.0 34.9 %collective-permute-start.15 = (bf16[128,2048]{1,0:T(8,128)(2,1)S(1)}, bf16[128,2048]{1,0:T(8,128)(2,1)S(1)}, u32[]{:S(2)}, u32[]{:S(2)}) collective-permute-start(bf16[128,2048]{1,0:T(8,128)(2,1)S(1)} %collective-permute-done.14.refs_12_), channel_id=1, source_target_pairs={{0,1},{1,0},{2,3},{3,2},{4,5},{5,4},{6,7},{7,6},{8,9},{9,8},{10,11... | collective-permute-start | bytes 1572872 | tf_op jit(solution)/shard_map/ppermute | solution.py:53
  14.2 36.8 %collective-permute-start.16 = (bf16[128,2048]{1,0:T(8,128)(2,1)S(1)}, bf16[128,2048]{1,0:T(8,128)(2,1)S(1)}, u32[]{:S(2)}, u32[]{:S(2)}) collective-permute-start(bf16[128,2048]{1,0:T(8,128)(2,1)S(1)} %collective-permute-done.14.refs_12_), channel_id=1, source_target_pairs={{0,2},{1,3},{2,0},{3,1},{4,6},{5,7},{6,4},{7,5},{8,10},{9,11},{10,... | collective-permute-start | bytes 1572872 | tf_op jit(solution)/shard_map/ppermute | solution.py:53
  33.3 35.4 %collective-permute-start.9 = (bf16[128,2048]{1,0:T(8,128)(2,1)S(1)}, bf16[128,2048]{1,0:T(8,128)(2,1)S(1)}, u32[]{:S(2)}, u32[]{:S(2)}) collective-permute-start(bf16[128,2048]{1,0:T(8,128)(2,1)S(1)} %either.2), channel_id=1, source_target_pairs={{0,2},{1,3},{2,0},{3,1},{4,5},{5,4},{6,7},{7,6},{8,10},{9,11},{10,... | collective-permute-start | bytes 1572872 | tf_op jit(solution)/shard_map/ppermute | solution.py:79
  33.7 8.3 %collective-permute-start.3 = (bf16[264,256]{1,0:T(8,128)(2,1)S(1)}, bf16[264,256]{1,0:T(8,128)(2,1)S(1)}, u32[]{:S(2)}, u32[]{:S(2)}) collective-permute-start(bf16[264,256]{1,0:T(8,128)(2,1)S(1)} %get-tuple-element.39), channel_id=1, source_target_pairs={{0,8},{4,12},{8,0},{12,4},{16,24},{20,28},{24,16},{28,20},{1,9},{5... | collective-permute-start | bytes 405512 | tf_op jit(solution)/shard_map/ppermute | solution.py:53
  41.9 23.5 %collective-permute-start.26 = (bf16[256,512]{1,0:T(8,128)(2,1)S(1)}, bf16[256,512]{1,0:T(8,128)(2,1)S(1)}, u32[]{:S(2)}, u32[]{:S(2)}) collective-permute-start(bf16[256,512]{1,0:T(8,128)(2,1)S(1)} %get-tuple-element.44.refs_0_.refs_6_), channel_id=1, source_target_pairs={{0,16},{4,20},{8,24},{12,28},{16,0},{20,4},{24,8},{28,12},{1,17},{... | collective-permute-start | bytes 786440 | tf_op jit(solution)/shard_map/ppermute | solution.py:53
  45.8 21.3 %collective-permute-start.25 = (bf16[256,512]{1,0:T(8,128)(2,1)S(1)}, bf16[256,512]{1,0:T(8,128)(2,1)S(1)}, u32[]{:S(2)}, u32[]{:S(2)}) collective-permute-start(bf16[256,512]{1,0:T(8,128)(2,1)S(1)} %get-tuple-element.45), channel_id=1, source_target_pairs={{0,8},{4,12},{8,0},{12,4},{16,24},{20,28},{24,16},{28,20},{1,9},{5... | collective-permute-start | bytes 786440 | tf_op jit(solution)/shard_map/ppermute | solution.py:53
  47.9 20.8 %collective-permute-start.27 = (bf16[256,512]{1,0:T(8,128)(2,1)S(1)}, bf16[256,512]{1,0:T(8,128)(2,1)S(1)}, u32[]{:S(2)}, u32[]{:S(2)}) collective-permute-start(bf16[256,512]{1,0:T(8,128)(2,1)S(1)} %get-tuple-element.45), channel_id=1, source_target_pairs={{0,24},{4,28},{8,16},{12,20},{16,8},{20,12},{24,0},{28,4},{1,25},{... | collective-permute-start | bytes 786440 | tf_op jit(solution)/shard_map/ppermute | solution.py:53
  51.0 18.3 %collective-permute-start.10 = (bf16[128,2048]{1,0:T(8,128)(2,1)}, bf16[128,2048]{1,0:T(8,128)(2,1)S(1)}, u32[]{:S(2)}, u32[]{:S(2)}) collective-permute-start(bf16[128,2048]{1,0:T(8,128)(2,1)} %refs_4_.3), channel_id=1, source_target_pairs={{0,4},{4,0},{8,12},{12,8},{16,20},{20,16},{24,28},{28,24},{1,5},{5... | collective-permute-start | bytes 1572872 | tf_op jit(solution)/shard_map/ppermute | solution.py:53
  65.5 8.1 %collective-permute-start.11 = (bf16[128,2048]{1,0:T(8,128)(2,1)S(1)}, bf16[128,2048]{1,0:T(8,128)(2,1)S(1)}, u32[]{:S(2)}, u32[]{:S(2)}) collective-permute-start(bf16[128,2048]{1,0:T(8,128)(2,1)S(1)} %collective-permute-done.7.refs_0_.refs_1_.refs_5_), channel_id=1, source_target_pairs={{0,4},{4,0},{8,12},{12,8},{16,20},{20,16},{24,28},{28,24},{1,5},{5... | collective-permute-start | bytes 1572872 | tf_op jit(solution)/shard_map/ppermute | solution.py:53
  68.7 8.4 %collective-permute-start.17 = (bf16[128,2048]{1,0:T(8,128)(2,1)S(1)}, bf16[128,2048]{1,0:T(8,128)(2,1)S(1)}, u32[]{:S(2)}, u32[]{:S(2)}) collective-permute-start(bf16[128,2048]{1,0:T(8,128)(2,1)S(1)} %either.3), channel_id=1, source_target_pairs={{0,2},{1,3},{2,0},{3,1},{4,5},{5,4},{6,7},{7,6},{8,10},{9,11},{10,... | collective-permute-start | bytes 1572872 | tf_op jit(solution)/shard_map/ppermute | solution.py:79
  69.3 13.6 %collective-permute-start.6 = (bf16[4,136,256]{2,1,0:T(8,128)(2,1)S(1)}, bf16[4,136,256]{2,1,0:T(8,128)(2,1)S(1)}, u32[]{:S(2)}, u32[]{:S(2)}) collective-permute-start(bf16[4,136,256]{2,1,0:T(8,128)(2,1)S(1)} %ssplit.1), channel_id=1, source_target_pairs={{0,4},{4,0},{8,12},{12,8},{16,20},{20,16},{24,28},{28,24},{1,5},{5... | collective-permute-start | bytes 835592 | tf_op jit(solution)/shard_map/ppermute | solution.py:53
  73.5 17.8 %collective-permute-start.18 = (bf16[128,2048]{1,0:T(8,128)(2,1)S(1)}, bf16[128,2048]{1,0:T(8,128)(2,1)S(1)}, u32[]{:S(2)}, u32[]{:S(2)}) collective-permute-start(bf16[128,2048]{1,0:T(8,128)(2,1)S(1)} %collective-permute-done.14.refs_12_), channel_id=1, source_target_pairs={{0,4},{4,0},{8,12},{12,8},{16,20},{20,16},{24,28},{28,24},{1,5},{5... | collective-permute-start | bytes 1572872 | tf_op jit(solution)/shard_map/ppermute | solution.py:53
  73.6 17.8 %collective-permute-start.19 = (bf16[128,2048]{1,0:T(8,128)(2,1)S(1)}, bf16[128,2048]{1,0:T(8,128)(2,1)S(1)}, u32[]{:S(2)}, u32[]{:S(2)}) collective-permute-start(bf16[128,2048]{1,0:T(8,128)(2,1)S(1)} %collective-permute-done.15.refs_0_.refs_13_), channel_id=1, source_target_pairs={{0,4},{4,0},{8,12},{12,8},{16,20},{20,16},{24,28},{28,24},{1,5},{5... | collective-permute-start | bytes 1572872 | tf_op jit(solution)/shard_map/ppermute | solution.py:53
  74.1 17.4 %collective-permute-start.20 = (bf16[128,2048]{1,0:T(8,128)(2,1)S(1)}, bf16[128,2048]{1,0:T(8,128)(2,1)S(1)}, u32[]{:S(2)}, u32[]{:S(2)}) collective-permute-start(bf16[128,2048]{1,0:T(8,128)(2,1)S(1)} %collective-permute-done.16.refs_1_.refs_14_), channel_id=1, source_target_pairs={{0,4},{4,0},{8,12},{12,8},{16,20},{20,16},{24,28},{28,24},{1,5},{5... | collective-permute-start | bytes 1572872 | tf_op jit(solution)/shard_map/ppermute | solution.py:53
  77.1 14.3 %collective-permute-start.21 = (bf16[128,2048]{1,0:T(8,128)(2,1)S(1)}, bf16[128,2048]{1,0:T(8,128)(2,1)S(1)}, u32[]{:S(2)}, u32[]{:S(2)}) collective-permute-start(bf16[128,2048]{1,0:T(8,128)(2,1)S(1)} %collective-permute-done.17.refs_15_), channel_id=1, source_target_pairs={{0,4},{4,0},{8,12},{12,8},{16,20},{20,16},{24,28},{28,24},{1,5},{5... | collective-permute-start | bytes 1572872 | tf_op jit(solution)/shard_map/ppermute | solution.py:53
  90.1 9.3 %collective-permute-start.29 = (bf16[256,512]{1,0:T(8,128)(2,1)S(1)}, bf16[256,512]{1,0:T(8,128)(2,1)S(1)}, u32[]{:S(2)}, u32[]{:S(2)}) collective-permute-start(bf16[256,512]{1,0:T(8,128)(2,1)S(1)} %get-tuple-element.49), channel_id=1, source_target_pairs={{0,4},{4,0},{8,12},{12,8},{16,20},{20,16},{24,28},{28,24},{1,5},{5... | collective-permute-start | bytes 786440 | tf_op jit(solution)/shard_map/ppermute | solution.py:53
  91.4 11.8 %collective-permute-start.28 = (bf16[4,256,256]{2,1,0:T(8,128)(2,1)S(1)}, bf16[4,256,256]{2,1,0:T(8,128)(2,1)S(1)}, u32[]{:S(2)}, u32[]{:S(2)}) collective-permute-start(bf16[4,256,256]{2,1,0:T(8,128)(2,1)S(1)} %xsplit.1), channel_id=1, source_target_pairs={{0,4},{4,0},{8,12},{12,8},{16,20},{20,16},{24,28},{28,24},{1,5},{5... | collective-permute-start | bytes 1572872 | tf_op jit(solution)/shard_map/ppermute | solution.py:53
  99.4 17.4 %collective-permute-start.30 = (bf16[512,256]{1,0:T(8,128)(2,1)S(1)}, bf16[512,256]{1,0:T(8,128)(2,1)S(1)}, u32[]{:S(2)}, u32[]{:S(2)}) collective-permute-start(bf16[512,256]{1,0:T(8,128)(2,1)S(1)} %pad_maximum_fusion.1), channel_id=1, source_target_pairs={{0,8},{4,12},{8,0},{12,4},{16,24},{20,28},{24,16},{28,20},{1,9},{5... | collective-permute-start | bytes 786440 | tf_op jit(solution)/shard_map/ppermute | solution.py:53
  99.5 20.1 %collective-permute-start.31 = (bf16[512,256]{1,0:T(8,128)(2,1)S(1)}, bf16[512,256]{1,0:T(8,128)(2,1)S(1)}, u32[]{:S(2)}, u32[]{:S(2)}) collective-permute-start(bf16[512,256]{1,0:T(8,128)(2,1)S(1)} %pad_maximum_fusion.refs_0_), channel_id=1, source_target_pairs={{0,16},{4,20},{8,24},{12,28},{16,0},{20,4},{24,8},{28,12},{1,17},{... | collective-permute-start | bytes 786440 | tf_op jit(solution)/shard_map/ppermute | solution.py:53
  99.6 20.0 %collective-permute-start.32 = (bf16[512,256]{1,0:T(8,128)(2,1)S(1)}, bf16[512,256]{1,0:T(8,128)(2,1)S(1)}, u32[]{:S(2)}, u32[]{:S(2)}) collective-permute-start(bf16[512,256]{1,0:T(8,128)(2,1)S(1)} %pad_maximum_fusion.1), channel_id=1, source_target_pairs={{0,24},{4,28},{8,16},{12,20},{16,8},{20,12},{24,0},{28,4},{1,25},{... | collective-permute-start | bytes 786440 | tf_op jit(solution)/shard_map/ppermute | solution.py:53
  115.5 12.6 %collective-permute-start.33 = (bf16[128,256]{1,0:T(8,128)(2,1)S(1)}, bf16[128,256]{1,0:T(8,128)(2,1)S(1)}, u32[]{:S(2)}, u32[]{:S(2)}) collective-permute-start(bf16[128,256]{1,0:T(8,128)(2,1)S(1)} %get-tuple-element.52), channel_id=1, source_target_pairs={{0,16},{4,20},{8,24},{12,28},{1,17},{5,21},{9,25},{13,29},{2,18},{... | collective-permute-start | bytes 196616 | tf_op jit(solution)/shard_map/ppermute | solution.py:719
  (21 other events, 164.9 us)

commit v2 on v1

--- a/solution.py
+++ b/solution.py
@@ -120,19 +120,16 @@
         opposite[c * rows : (c + 1) * rows] = side_columns(held.at[c], 1, 1 - place[4], pair)
 
 
-def prepare_kernel(heads_mine, place, *refs):
-    inputs, outs, held, sems = refs[:7], refs[7:17], refs[17:24], refs[24]
+def prepare_kernel(place, *refs):
+    inputs, outs, held, sems = refs[:2], refs[2:5], refs[5:7], refs[7]
     copies = [pltpu.make_async_copy(a, b, sems.at[i]) for i, (a, b) in enumerate(zip(inputs, held))]
     for copy in copies:
         copy.start()
-    project, state, step, taps, mixer_taps, step_bias, decay_log = held
-    for copy in copies[1:]:
+    state, step = held
+    state_turned, step_same, step_opposite = outs
+    side = place[4]
+    for copy in copies:
         copy.wait()
-    gate_same, gate_opposite, gate_sent, state_turned, step_same, step_opposite, taps_state = outs[:7]
-    taps_mixer, bias, rate = outs[7:]
-    side, core = place[4], place[3]
-    width = gate_same.shape[1]
-
     cols = state.shape[2]
     target = lax.broadcasted_iota(jnp.int32, (2 * cols, cols), 0)
     source = lax.broadcasted_iota(jnp.int32, (2 * cols, cols), 1)
@@ -147,19 +144,35 @@
             preferred_element_type=F32,
         )
     state_turned[...] = turned.astype(BF16)
-    heads = step.shape[0]
-    half = heads // 2
+    half = step.shape[0] // 2
     turned_step = jnp.concatenate([step[...].astype(F32), jnp.zeros((PAD, step.shape[1]), F32)], axis=0)
     low = turned_step[:PAD]
     high = turned_step[half : half + PAD]
     step_same[...] = jnp.where(side == 0, low, high).astype(BF16)
     step_opposite[...] = jnp.where(side == 0, high, low).astype(BF16)
+
+
+def settings_kernel(heads_mine, place, *refs):
+    inputs, outs, held, sems = refs[:5], refs[5:12], refs[12:17], refs[17]
+    copies = [pltpu.make_async_copy(a, b, sems.at[i]) for i, (a, b) in enumerate(zip(inputs, held))]
+    for copy in copies:
+        copy.start()
+    project, taps, mixer_taps, step_bias, decay_log = held
+    for copy in copies:
+        copy.wait()
+    gate_same, gate_opposite, gate_sent, taps_state, taps_mixer, bias, rate = outs
+    quarter, core, side = place[0], place[3], place[4]
+    width = gate_same.shape[1]
+    other_side = 1 - side
+    gate_same[...] = side_columns(project, 0, 2 * side + core, width)
+    gate_opposite[...] = side_columns(project, 0, 2 * other_side + core, width)
+    gate_sent[:, :width] = side_columns(project, 0, 2 * side + 1 - core, width)
+    gate_sent[:, width:] = side_columns(project, 0, 2 * other_side + 1 - core, width)
     source = lax.broadcasted_iota(jnp.int32, (taps.shape[2], N), 0)
     target = lax.broadcasted_iota(jnp.int32, (taps.shape[2], N), 1)
     chosen = (source == target * G + place[5]).astype(F32)
     mine = jnp.where(core == 0, taps[:, 0, :], taps[:, 1, :])
     taps_state[: CONV + 1] = exact_dot(mine, chosen, ((1,), (0,)))
-    quarter = place[0]
     if width % LANES == 0:
         taps_mixer[: CONV + 1] = mixer_taps[:, pl.ds(pl.multiple_of(quarter * width, width), width)]
     else:
@@ -167,18 +180,13 @@
         for k in range(1, TEAM):
             got = jnp.where(quarter == k, mixer_taps[:, k * width : (k + 1) * width], got)
         taps_mixer[: CONV + 1] = got
+    heads = step_bias.shape[1]
     row = lax.broadcasted_iota(jnp.int32, (PAD, heads), 0)
     column = lax.broadcasted_iota(jnp.int32, (PAD, heads), 1)
     own = jnp.logical_and(column == quarter * heads_mine + row, row < heads_mine)
     for values, out in ((step_bias[...], bias), (-jnp.exp(decay_log[...]), rate)):
         picked = jnp.sum(jnp.where(own, values, 0.0), axis=1, keepdims=True)
         out[...] = jnp.broadcast_to(picked, out.shape)
-    copies[0].wait()
-    other_side = 1 - side
-    gate_same[...] = side_columns(project, 0, 2 * side + core, width)
-    gate_opposite[...] = side_columns(project, 0, 2 * other_side + core, width)
-    gate_sent[:, :width] = side_columns(project, 0, 2 * side + 1 - core, width)
-    gate_sent[:, width:] = side_columns(project, 0, 2 * other_side + 1 - core, width)
 
 
 def either_kernel(place, first, second, out, sem):
@@ -522,7 +530,12 @@
     partner = swapped(tokens, "ctx", 2)
     near = inner_blocks(tokens, at, inner_count, ctx_count)
     beyond = inner_blocks(partner, at, inner_count, ctx_count)
-    blocks = near + [swapped(b, "ctx", 1) for b in near] + beyond + [swapped(b, "ctx", 1) for b in beyond]
+    blocks = (
+        near
+        + [swapped(b, "ctx", 1) for b in near]
+        + beyond
+        + [swapped(b, "ctx", 1) for b in beyond]
+    )
     tail = pl.pallas_call(
         at(tail_kernel),
         in_specs=[ANY] * (2 * inner_count),
@@ -554,37 +567,49 @@
         compiler_params=SMALL,
         name="columns",
     )(project_weight)
-    to_prepare = (
+
+    def held_in_vmem(values):
+        return [pltpu.VMEM(v.shape, v.dtype) for v in values] + [pltpu.SemaphoreType.DMA((len(values),))]
+
+    to_prepare = (state_weight, step_weight.T)
+    state_turned, *step_sides = pl.pallas_call(
+        at(prepare_kernel),
+        in_specs=[HBM] * 2,
+        out_specs=[VMEM] * 3,
+        out_shape=[
+            sds((2 * slice_cols, rows_here), BF16),
+            sds((PAD, rows_here), BF16),
+            sds((PAD, rows_here), BF16),
+        ],
+        scratch_shapes=held_in_vmem(to_prepare),
+        compiler_params=SMALL,
+        name="prepare",
+    )(*to_prepare)
+    to_set = (
         project_weight,
-        state_weight,
-        step_weight.T,
         state_taps,
         mixer_taps,
         step_bias.reshape(1, -1),
         decay_log.reshape(1, -1),
     )
-    prepared = pl.pallas_call(
-        at(functools.partial(prepare_kernel, heads_mine)),
-        in_specs=[HBM] * 7,
-        out_specs=[VMEM] * 10,
+    settings = pl.pallas_call(
+        at(functools.partial(settings_kernel, heads_mine)),
+        in_specs=[HBM] * 5,
+        out_specs=[VMEM] * 7,
         out_shape=[
             sds((rows_here, width_mine), BF16),
             sds((rows_here, width_mine), BF16),
             sds((rows_here, pair), BF16),
-            sds((2 * slice_cols, rows_here), BF16),
-            sds((PAD, rows_here), BF16),
-            sds((PAD, rows_here), BF16),
             sds((PAD, N), F32),
             sds((PAD, width_mine), F32),
             sds((PAD, SPAN), F32),
             sds((PAD, SPAN), F32),
         ],
-        scratch_shapes=[pltpu.VMEM(v.shape, v.dtype) for v in to_prepare] + [pltpu.SemaphoreType.DMA((7,))],
+        scratch_shapes=held_in_vmem(to_set),
         compiler_params=SMALL,
-        name="prepare",
-    )(*to_prepare)
-    gate_mine, gate_sent = prepared[0:2], prepared[2]
-    state_turned, step_sides = prepared[3], prepared[4:6]
+        name="settings",
+    )(*to_set)
+    gate_mine, gate_sent = settings[:2], settings[2]
 
     x_pieces = gathered_rows(lambda d: x_sides[d % 2], z_count)
 
@@ -661,7 +686,7 @@
     ]
     gate_pieces = gathered_rows(lambda d: gate_chip[d % 2], z_count)
 
-    taps_state, taps_mine, bias_mine, rate_mine = prepared[6:]
+    taps_state, taps_mine, bias_mine, rate_mine = settings[3:]
 
     shared = total * model_width <= 2**23
     tok_shape = (HALO + total, model_width)
@@ -764,4 +789,6 @@
         P(),
     )
 
-    return jax.shard_map(on_device, mesh=mesh, in_specs=placed, out_specs=P(("ctx", "inner"), None), check_vma=False)
+    return jax.shard_map(
+        on_device, mesh=mesh, in_specs=placed, out_specs=P(("ctx", "inner"), None), check_vma=False
+    )

time: 160 us -> 160 us (level)
  local copies, waits for them, and re-layouts: 7.91 us -> 3.91 us
  waiting for transfers between devices: 43.2 us -> 45.5 us
    unnamed x22, local copies, waits for them, and re-layouts: 7.89 us -> 3.89 us
    ppermute x2, waiting for transfers between devices: 2.97 us -> 5.64 us  [inner_blocks(): far = lax.ppermute(onward, ('ctx', 'inner'), pairs)]
  transfers between devices with their start and end apart: 34 -> 34, of which waited for: 10 -> 10; matrix products, arithmetic and copies ran while one was open for 0% -> 0% of each run, Pallas kernels for 17% -> 18%
where the time goes in v2:
time: 160 us; the launch traced here: 158 us
  starting transfers between devices  49.9 us (31%)
  waiting for transfers between devices  45.5 us (28%)
  Pallas kernels  35.6 us (22%)
  blocking collectives  22.6 us (14%)
  local copies, waits for them, and re-layouts  3.91 us (2%)
    ppermute x29, starting transfers between devices, swapped(): return lax.ppermute(x, axis, pairs)  45.1 us
    ppermute x29, waiting for transfers between devices, swapped(): return lax.ppermute(x, axis, pairs)  31.1 us
    all_to_all x1, blocking collectives, on_device(): lax.all_to_all(gated, ('ctx', 'inner'), 0, 0, axis_index_groups=teams, ti...  22.6 us
    pallas_call x1, Pallas kernels, on_device(): pl.pallas_call(at(functools.partial(mixer_kernel, inner_count, shared, z_...  12.3 us
    pallas_call x1, Pallas kernels, on_device(): pl.pallas_call(at(functools.partial(state_kernel, inner_count)), in_specs...  7.35 us
    pallas_call x1, Pallas kernels, on_device(): pl.pallas_call(at(scan_kernel), in_specs=[VMEM] * 8, out_specs=VMEM, out_...  6.03 us
    ppermute x2, waiting for transfers between devices, inner_blocks(): far = lax.ppermute(onward, ('ctx', 'inner'), pairs)  5.64 us
    ppermute x2, waiting for transfers between devices, on_device(): halo = halo + lax.ppermute(tail, 'ctx', pairs)  4.64 us
  transfers between devices with their start and end apart: 34, of which 10 were waited for; matrix products, arithmetic and copies ran while one was open for 0% of the time, Pallas kernels for 18%

profile of v2, /device:TPU:25, one launch (start us, length us, event | category | flops | bytes accessed | tf_op | source)
XLA Modules:
  0.0 158.0 jit_solution(9113238671273425085)
XLA Ops:
  2.6 10.4 %collective-permute-done.14.refs_12_ = bf16[128,2048]{1,0:T(8,128)(2,1)S(1)} collective-permute-done((bf16[128,2048]{1,0:T(8,128)(2,1)}, bf16[128,2048]{1,0:T(8,128)(2,1)S(1)}, u32[]{:S(2)}, u32[]{:S(2)}) %collective-permute-start.14) | collective-permute-done | bytes 524320 | tf_op jit(solution)/shard_map/ppermute | solution.py:53
  18.1 7.5 %collective-permute-done.refs_1_ = bf16[64,256]{1,0:T(8,128)(2,1)S(1)} collective-permute-done((bf16[64,256]{1,0:T(8,128)(2,1)S(1)}, bf16[64,256]{1,0:T(8,128)(2,1)S(1)}, u32[]{:S(2)}, u32[]{:S(2)}) %collective-permute-start) | collective-permute-done | bytes 32800 | tf_op jit(solution)/shard_map/ppermute | solution.py:53
  26.9 1.5 collective-permute-done.1.refs_2_
  28.4 2.2 %collective-permute-start.2 = (bf16[64,256]{1,0:T(8,128)(2,1)S(1)}, bf16[64,256]{1,0:T(8,128)(2,1)S(1)}, u32[]{:S(2)}, u32[]{:S(2)}) collective-permute-start(bf16[64,256]{1,0:T(8,128)(2,1)S(1)} %get-tuple-element.35), channel_id=1, source_target_pairs={{0,3},{1,2},{2,1},{3,0},{4,7},{5,6},{6,5},{7,4},{8,11},{9,10},{10,... | collective-permute-start | bytes 98312 | tf_op jit(solution)/shard_map/ppermute | solution.py:53
  30.6 1.5 collective-permute-done.2.refs_3_
  33.8 4.6 %collective-permute-done.4.refs_2_.refs_3_ = bf16[264,256]{1,0:T(8,128)(2,1)S(1)} collective-permute-done((bf16[264,256]{1,0:T(8,128)(2,1)S(1)}, bf16[264,256]{1,0:T(8,128)(2,1)S(1)}, u32[]{:S(2)}, u32[]{:S(2)}) %collective-permute-start.4) | collective-permute-done | bytes 135200 | tf_op jit(solution)/shard_map/ppermute | solution.py:53
  41.4 2.7 %collective-permute-done.5.refs_3_.refs_4_ = bf16[264,256]{1,0:T(8,128)(2,1)S(1)} collective-permute-done((bf16[264,256]{1,0:T(8,128)(2,1)S(1)}, bf16[264,256]{1,0:T(8,128)(2,1)S(1)}, u32[]{:S(2)}, u32[]{:S(2)}) %collective-permute-start.5) | collective-permute-done | bytes 135200 | tf_op jit(solution)/shard_map/ppermute | solution.py:53
  44.2 2.7 %collective-permute-start.25 = (bf16[256,512]{1,0:T(8,128)(2,1)S(1)}, bf16[256,512]{1,0:T(8,128)(2,1)S(1)}, u32[]{:S(2)}, u32[]{:S(2)}) collective-permute-start(bf16[256,512]{1,0:T(8,128)(2,1)S(1)} %get-tuple-element.45), channel_id=1, source_target_pairs={{0,8},{4,12},{8,0},{12,4},{16,24},{20,28},{24,16},{28,20},{1,9},{5... | collective-permute-start | bytes 786440 | tf_op jit(solution)/shard_map/ppermute | solution.py:53
  46.9 3.1 %collective-permute-start.27 = (bf16[256,512]{1,0:T(8,128)(2,1)S(1)}, bf16[256,512]{1,0:T(8,128)(2,1)S(1)}, u32[]{:S(2)}, u32[]{:S(2)}) collective-permute-start(bf16[256,512]{1,0:T(8,128)(2,1)S(1)} %get-tuple-element.45), channel_id=1, source_target_pairs={{0,24},{4,28},{8,16},{12,20},{16,8},{20,12},{24,0},{28,4},{1,25},{... | collective-permute-start | bytes 786440 | tf_op jit(solution)/shard_map/ppermute | solution.py:53
  50.0 8.3 %collective-permute-start.10 = (bf16[128,2048]{1,0:T(8,128)(2,1)}, bf16[128,2048]{1,0:T(8,128)(2,1)S(1)}, u32[]{:S(2)}, u32[]{:S(2)}) collective-permute-start(bf16[128,2048]{1,0:T(8,128)(2,1)} %refs_4_.1), channel_id=1, source_target_pairs={{0,4},{4,0},{8,12},{12,8},{16,20},{20,16},{24,28},{28,24},{1,5},{5... | collective-permute-start | bytes 1572872 | tf_op jit(solution)/shard_map/ppermute | solution.py:53
  58.4 10.3 %collective-permute-start.11 = (bf16[128,2048]{1,0:T(8,128)(2,1)S(1)}, bf16[128,2048]{1,0:T(8,128)(2,1)S(1)}, u32[]{:S(2)}, u32[]{:S(2)}) collective-permute-start(bf16[128,2048]{1,0:T(8,128)(2,1)S(1)} %collective-permute-done.7.refs_0_.refs_1_.refs_5_), channel_id=1, source_target_pairs={{0,4},{4,0},{8,12},{12,8},{16,20},{20,16},{24,28},{28,24},{1,5},{5... | collective-permute-start | bytes 1572872 | tf_op jit(solution)/shard_map/ppermute | solution.py:53
  69.9 2.0 %collective-permute-start.6 = (bf16[4,136,256]{2,1,0:T(8,128)(2,1)S(1)}, bf16[4,136,256]{2,1,0:T(8,128)(2,1)S(1)}, u32[]{:S(2)}, u32[]{:S(2)}) collective-permute-start(bf16[4,136,256]{2,1,0:T(8,128)(2,1)S(1)} %ssplit.1), channel_id=1, source_target_pairs={{0,4},{4,0},{8,12},{12,8},{16,20},{20,16},{24,28},{28,24},{1,5},{5... | collective-permute-start | bytes 835592 | tf_op jit(solution)/shard_map/ppermute | solution.py:53
  72.5 5.6 %collective-permute-done.17.refs_15_ = bf16[128,2048]{1,0:T(8,128)(2,1)S(1)} collective-permute-done((bf16[128,2048]{1,0:T(8,128)(2,1)S(1)}, bf16[128,2048]{1,0:T(8,128)(2,1)S(1)}, u32[]{:S(2)}, u32[]{:S(2)}) %collective-permute-start.17) | collective-permute-done | bytes 524320 | tf_op jit(solution)/shard_map/ppermute | solution.py:79
  82.8 2.0 %settings.1 = (bf16[256,256]{1,0:T(8,128)(2,1)S(1)}, bf16[256,256]{1,0:T(8,128)(2,1)S(1)}, bf16[256,512]{1,0:T(8,128)(2,1)S(1)}, f32[8,128]{1,0:T(8,128)S(1)}, f...) custom-call(bf16[256,2,1024]{2,1,0:T(2,128)(2,1)S(1)} %copy-done.1, f32[5,2,512]{2,1,0:T(2,128)S(1)} %copy-done.6, ...), custom_call_target="tpu_custom_call" | custom-call | tf_op jit(solution)/shard_map/settings/pallas_call | solution.py:595
  84.8 4.6 %collective-permute-done.23 = bf16[16,2048]{1,0:T(8,128)(2,1)S(1)} collective-permute-done((bf16[16,2048]{1,0:T(8,128)(2,1)S(1)}, bf16[16,2048]{1,0:T(8,128)(2,1)S(1)}, u32[]{:S(2)}, u32[]{:S(2)}) %collective-permute-start.23) | collective-permute-done | bytes 65568 | tf_op jit(solution)/shard_map/ppermute | solution.py:553
  89.5 1.7 %collective-permute-start.29 = (bf16[256,512]{1,0:T(8,128)(2,1)S(1)}, bf16[256,512]{1,0:T(8,128)(2,1)S(1)}, u32[]{:S(2)}, u32[]{:S(2)}) collective-permute-start(bf16[256,512]{1,0:T(8,128)(2,1)S(1)} %get-tuple-element.49), channel_id=1, source_target_pairs={{0,4},{4,0},{8,12},{12,8},{16,20},{20,16},{24,28},{28,24},{1,5},{5... | collective-permute-start | bytes 786440 | tf_op jit(solution)/shard_map/ppermute | solution.py:53
  91.7 7.3 %state.1 = (bf16[2048,128]{1,0:T(8,128)(2,1)S(1)}, f32[16,8,128]{2,1,0:T(8,128)S(1)}, f32[16,8,128]{2,1,0:T(8,128)S(1)}, bf16[2064,2048]{1,0:T(8,128)(2,1)S(1)}) custom-call(f32[8,128]{1,0:T(8,128)S(1)} %get-tuple-element.29.refs_0_, f32[8,128]{1,0:T(8,128)S(1)} %get-tuple-element.30.refs_1_, f32[8,128]{1,0:T(8,128)S(1)} %get-tuple-element.31.refs_2_, ...), custom_call_target="tpu_custom_call" | custom-call | tf_op jit(solution)/shard_map/state/pallas_call | solution.py:707
  100.0 3.4 %collective-permute-start.32 = (bf16[512,256]{1,0:T(8,128)(2,1)S(1)}, bf16[512,256]{1,0:T(8,128)(2,1)S(1)}, u32[]{:S(2)}, u32[]{:S(2)}) collective-permute-start(bf16[512,256]{1,0:T(8,128)(2,1)S(1)} %pad_maximum_fusion.1), channel_id=1, source_target_pairs={{0,24},{4,28},{8,16},{12,20},{16,8},{20,12},{24,0},{28,4},{1,25},{... | collective-permute-start | bytes 786440 | tf_op jit(solution)/shard_map/ppermute | solution.py:53
  103.4 12.3 %mixer.1 = (bf16[2048,256]{1,0:T(8,128)(2,1)S(1)}, f32[16,128,256]{2,1,0:T(8,128)S(1)}, bf16[128,256]{1,0:T(8,128)(2,1)S(1)}, f32[8,256]{1,0:T(8,128)}) custom-call(f32[8,256]{1,0:T(8,128)S(1)} %get-tuple-element.41.refs_0_, bf16[2048,128]{1,0:T(8,128)(2,1)S(1)} %get-tuple-element.40.refs_1_.refs_0_, ...), custom_call_target="tpu_custom_call" | custom-call | tf_op jit(solution)/shard_map/mixer/pallas_call | solution.py:722
  117.0 2.7 %collective-permute-done.31.refs_2_ = bf16[512,256]{1,0:T(8,128)(2,1)S(1)} collective-permute-done((bf16[512,256]{1,0:T(8,128)(2,1)S(1)}, bf16[512,256]{1,0:T(8,128)(2,1)S(1)}, u32[]{:S(2)}, u32[]{:S(2)}) %collective-permute-start.31) | collective-permute-done | bytes 262176 | tf_op jit(solution)/shard_map/ppermute | solution.py:53
  119.7 4.0 %gate.1.refs_3_ = bf16[2048,256]{1,0:T(8,128)(2,1)S(1)} custom-call(bf16[512,256]{1,0:T(8,128)(2,1)S(1)} %pad_maximum_fusion.refs_0_, bf16[512,256]{1,0:T(8,128)(2,1)S(1)} %collective-permute-done.30.refs_1_, bf16[512,256]{1,0:T(8,128)(2,1)S(1)} %collective-permute-done.31.refs_2_, bf16[512,256]{1,0:T(8,128)(2,1)S(1)} %collective-permute-done.32.refs_3_, ...), custom_call_target="tpu_custom_call" | custom-call | tf_op jit(solution)/shard_map/gate/pallas_call | solution.py:746
  123.7 4.2 %collective-permute-done.33.refs_7_ = bf16[128,256]{1,0:T(8,128)(2,1)S(1)} collective-permute-done((bf16[128,256]{1,0:T(8,128)(2,1)S(1)}, bf16[128,256]{1,0:T(8,128)(2,1)S(1)}, u32[]{:S(2)}, u32[]{:S(2)}) %collective-permute-start.33) | collective-permute-done | bytes 65568 | tf_op jit(solution)/shard_map/ppermute | solution.py:744
  127.9 6.0 %scan.1 = bf16[2048,256]{1,0:T(8,128)(2,1)S(1)} custom-call(bf16[2048,128]{1,0:T(8,128)(2,1)S(1)} %get-tuple-element.40.refs_1_.refs_0_, bf16[2048,128]{1,0:T(8,128)(2,1)S(1)} %collective-permute-done.24.refs_2_.refs_1_, bf16[2048,256]{1,0:T(8,128)(2,1)S(1)} %get-tuple-element.47.refs_2_, bf16[2048,256]{1,0:T(8,128)(2,1)S(1)} %gate.1.refs_3_, ...), custom_call_target="tpu_custom_call" | custom-call | tf_op jit(solution)/shard_map/scan/pallas_call | solution.py:756
  133.9 22.6 %all_to_all.9.refs_0_ = bf16[16,128,256]{2,1,0:T(8,128)(2,1)S(1)} all-to-all(bf16[16,128,256]{2,1,0:T(8,128)(2,1)S(1)} %bitcast.5), channel_id=1, replica_groups={{0,1,2,3,4,5,6,7,8,9,10,11,12,13,14,15},{16,17,18,19,20,21,22,23,24,25,..., dimensions={0} | all-to-all | bytes 2097152 | tf_op jit(solution)/shard_map/all_to_all | solution.py:766
  (87 shorter events, 24.3 us)
Async XLA Ops:
  0.0 13.0 %collective-permute-start.14 = (bf16[128,2048]{1,0:T(8,128)(2,1)}, bf16[128,2048]{1,0:T(8,128)(2,1)S(1)}, u32[]{:S(2)}, u32[]{:S(2)}) collective-permute-start(bf16[128,2048]{1,0:T(8,128)(2,1)} %refs_4_.1), channel_id=1, source_target_pairs={{0,8},{4,12},{8,0},{12,4},{16,24},{20,28},{24,16},{28,20},{1,9},{5... | collective-permute-start | bytes 1572872 | tf_op jit(solution)/shard_map/ppermute | solution.py:53
  0.2 32.1 %collective-permute-start.7 = (bf16[128,2048]{1,0:T(8,128)(2,1)}, bf16[128,2048]{1,0:T(8,128)(2,1)S(1)}, u32[]{:S(2)}, u32[]{:S(2)}) collective-permute-start(bf16[128,2048]{1,0:T(8,128)(2,1)} %refs_4_.1), channel_id=1, source_target_pairs={{0,1},{1,0},{2,3},{3,2},{4,5},{5,4},{6,7},{7,6},{8,9},{9,8},{10,11... | collective-permute-start | bytes 1572872 | tf_op jit(solution)/shard_map/ppermute | solution.py:53
  1.4 30.9 %collective-permute-start.8 = (bf16[128,2048]{1,0:T(8,128)(2,1)}, bf16[128,2048]{1,0:T(8,128)(2,1)S(1)}, u32[]{:S(2)}, u32[]{:S(2)}) collective-permute-start(bf16[128,2048]{1,0:T(8,128)(2,1)} %refs_4_.1), channel_id=1, source_target_pairs={{0,2},{1,3},{2,0},{3,1},{4,6},{5,7},{6,4},{7,5},{8,10},{9,11},{10,... | collective-permute-start | bytes 1572872 | tf_op jit(solution)/shard_map/ppermute | solution.py:53
  13.0 33.8 %collective-permute-start.15 = (bf16[128,2048]{1,0:T(8,128)(2,1)S(1)}, bf16[128,2048]{1,0:T(8,128)(2,1)S(1)}, u32[]{:S(2)}, u32[]{:S(2)}) collective-permute-start(bf16[128,2048]{1,0:T(8,128)(2,1)S(1)} %collective-permute-done.14.refs_12_), channel_id=1, source_target_pairs={{0,1},{1,0},{2,3},{3,2},{4,5},{5,4},{6,7},{7,6},{8,9},{9,8},{10,11... | collective-permute-start | bytes 1572872 | tf_op jit(solution)/shard_map/ppermute | solution.py:53
  14.2 35.7 %collective-permute-start.16 = (bf16[128,2048]{1,0:T(8,128)(2,1)S(1)}, bf16[128,2048]{1,0:T(8,128)(2,1)S(1)}, u32[]{:S(2)}, u32[]{:S(2)}) collective-permute-start(bf16[128,2048]{1,0:T(8,128)(2,1)S(1)} %collective-permute-done.14.refs_12_), channel_id=1, source_target_pairs={{0,2},{1,3},{2,0},{3,1},{4,6},{5,7},{6,4},{7,5},{8,10},{9,11},{10,... | collective-permute-start | bytes 1572872 | tf_op jit(solution)/shard_map/ppermute | solution.py:53
  32.3 37.5 %collective-permute-start.9 = (bf16[128,2048]{1,0:T(8,128)(2,1)S(1)}, bf16[128,2048]{1,0:T(8,128)(2,1)S(1)}, u32[]{:S(2)}, u32[]{:S(2)}) collective-permute-start(bf16[128,2048]{1,0:T(8,128)(2,1)S(1)} %either.2), channel_id=1, source_target_pairs={{0,2},{1,3},{2,0},{3,1},{4,5},{5,4},{6,7},{7,6},{8,10},{9,11},{10,... | collective-permute-start | bytes 1572872 | tf_op jit(solution)/shard_map/ppermute | solution.py:79
  41.4 17.0 %collective-permute-start.26 = (bf16[256,512]{1,0:T(8,128)(2,1)S(1)}, bf16[256,512]{1,0:T(8,128)(2,1)S(1)}, u32[]{:S(2)}, u32[]{:S(2)}) collective-permute-start(bf16[256,512]{1,0:T(8,128)(2,1)S(1)} %get-tuple-element.44.refs_0_.refs_6_), channel_id=1, source_target_pairs={{0,16},{4,20},{8,24},{12,28},{16,0},{20,4},{24,8},{28,12},{1,17},{... | collective-permute-start | bytes 786440 | tf_op jit(solution)/shard_map/ppermute | solution.py:53
  44.2 24.5 %collective-permute-start.25 = (bf16[256,512]{1,0:T(8,128)(2,1)S(1)}, bf16[256,512]{1,0:T(8,128)(2,1)S(1)}, u32[]{:S(2)}, u32[]{:S(2)}) collective-permute-start(bf16[256,512]{1,0:T(8,128)(2,1)S(1)} %get-tuple-element.45), channel_id=1, source_target_pairs={{0,8},{4,12},{8,0},{12,4},{16,24},{20,28},{24,16},{28,20},{1,9},{5... | collective-permute-start | bytes 786440 | tf_op jit(solution)/shard_map/ppermute | solution.py:53
  46.9 22.9 %collective-permute-start.27 = (bf16[256,512]{1,0:T(8,128)(2,1)S(1)}, bf16[256,512]{1,0:T(8,128)(2,1)S(1)}, u32[]{:S(2)}, u32[]{:S(2)}) collective-permute-start(bf16[256,512]{1,0:T(8,128)(2,1)S(1)} %get-tuple-element.45), channel_id=1, source_target_pairs={{0,24},{4,28},{8,16},{12,20},{16,8},{20,12},{24,0},{28,4},{1,25},{... | collective-permute-start | bytes 786440 | tf_op jit(solution)/shard_map/ppermute | solution.py:53
  50.0 19.9 %collective-permute-start.10 = (bf16[128,2048]{1,0:T(8,128)(2,1)}, bf16[128,2048]{1,0:T(8,128)(2,1)S(1)}, u32[]{:S(2)}, u32[]{:S(2)}) collective-permute-start(bf16[128,2048]{1,0:T(8,128)(2,1)} %refs_4_.1), channel_id=1, source_target_pairs={{0,4},{4,0},{8,12},{12,8},{16,20},{20,16},{24,28},{28,24},{1,5},{5... | collective-permute-start | bytes 1572872 | tf_op jit(solution)/shard_map/ppermute | solution.py:53
  58.4 13.6 %collective-permute-start.11 = (bf16[128,2048]{1,0:T(8,128)(2,1)S(1)}, bf16[128,2048]{1,0:T(8,128)(2,1)S(1)}, u32[]{:S(2)}, u32[]{:S(2)}) collective-permute-start(bf16[128,2048]{1,0:T(8,128)(2,1)S(1)} %collective-permute-done.7.refs_0_.refs_1_.refs_5_), channel_id=1, source_target_pairs={{0,4},{4,0},{8,12},{12,8},{16,20},{20,16},{24,28},{28,24},{1,5},{5... | collective-permute-start | bytes 1572872 | tf_op jit(solution)/shard_map/ppermute | solution.py:53
  69.8 8.4 %collective-permute-start.17 = (bf16[128,2048]{1,0:T(8,128)(2,1)S(1)}, bf16[128,2048]{1,0:T(8,128)(2,1)S(1)}, u32[]{:S(2)}, u32[]{:S(2)}) collective-permute-start(bf16[128,2048]{1,0:T(8,128)(2,1)S(1)} %either.3), channel_id=1, source_target_pairs={{0,2},{1,3},{2,0},{3,1},{4,5},{5,4},{6,7},{7,6},{8,10},{9,11},{10,... | collective-permute-start | bytes 1572872 | tf_op jit(solution)/shard_map/ppermute | solution.py:79
  69.9 10.7 %collective-permute-start.6 = (bf16[4,136,256]{2,1,0:T(8,128)(2,1)S(1)}, bf16[4,136,256]{2,1,0:T(8,128)(2,1)S(1)}, u32[]{:S(2)}, u32[]{:S(2)}) collective-permute-start(bf16[4,136,256]{2,1,0:T(8,128)(2,1)S(1)} %ssplit.1), channel_id=1, source_target_pairs={{0,4},{4,0},{8,12},{12,8},{16,20},{20,16},{24,28},{28,24},{1,5},{5... | collective-permute-start | bytes 835592 | tf_op jit(solution)/shard_map/ppermute | solution.py:53
  71.9 19.7 %collective-permute-start.18 = (bf16[128,2048]{1,0:T(8,128)(2,1)S(1)}, bf16[128,2048]{1,0:T(8,128)(2,1)S(1)}, u32[]{:S(2)}, u32[]{:S(2)}) collective-permute-start(bf16[128,2048]{1,0:T(8,128)(2,1)S(1)} %collective-permute-done.14.refs_12_), channel_id=1, source_target_pairs={{0,4},{4,0},{8,12},{12,8},{16,20},{20,16},{24,28},{28,24},{1,5},{5... | collective-permute-start | bytes 1572872 | tf_op jit(solution)/shard_map/ppermute | solution.py:53
  72.0 19.7 %collective-permute-start.19 = (bf16[128,2048]{1,0:T(8,128)(2,1)S(1)}, bf16[128,2048]{1,0:T(8,128)(2,1)S(1)}, u32[]{:S(2)}, u32[]{:S(2)}) collective-permute-start(bf16[128,2048]{1,0:T(8,128)(2,1)S(1)} %collective-permute-done.15.refs_0_.refs_13_), channel_id=1, source_target_pairs={{0,4},{4,0},{8,12},{12,8},{16,20},{20,16},{24,28},{28,24},{1,5},{5... | collective-permute-start | bytes 1572872 | tf_op jit(solution)/shard_map/ppermute | solution.py:53
  72.5 19.2 %collective-permute-start.20 = (bf16[128,2048]{1,0:T(8,128)(2,1)S(1)}, bf16[128,2048]{1,0:T(8,128)(2,1)S(1)}, u32[]{:S(2)}, u32[]{:S(2)}) collective-permute-start(bf16[128,2048]{1,0:T(8,128)(2,1)S(1)} %collective-permute-done.16.refs_1_.refs_14_), channel_id=1, source_target_pairs={{0,4},{4,0},{8,12},{12,8},{16,20},{20,16},{24,28},{28,24},{1,5},{5... | collective-permute-start | bytes 1572872 | tf_op jit(solution)/shard_map/ppermute | solution.py:53
  78.2 13.5 %collective-permute-start.21 = (bf16[128,2048]{1,0:T(8,128)(2,1)S(1)}, bf16[128,2048]{1,0:T(8,128)(2,1)S(1)}, u32[]{:S(2)}, u32[]{:S(2)}) collective-permute-start(bf16[128,2048]{1,0:T(8,128)(2,1)S(1)} %collective-permute-done.17.refs_15_), channel_id=1, source_target_pairs={{0,4},{4,0},{8,12},{12,8},{16,20},{20,16},{24,28},{28,24},{1,5},{5... | collective-permute-start | bytes 1572872 | tf_op jit(solution)/shard_map/ppermute | solution.py:53
  81.3 8.2 %collective-permute-start.23 = (bf16[16,2048]{1,0:T(8,128)(2,1)S(1)}, bf16[16,2048]{1,0:T(8,128)(2,1)S(1)}, u32[]{:S(2)}, u32[]{:S(2)}) collective-permute-start(bf16[16,2048]{1,0:T(8,128)(2,1)S(1)} %tail.1), channel_id=1, source_target_pairs={{8,24},{12,28},{9,25},{13,29},{10,26},{14,30},{11,27},{15,31}} | collective-permute-start | bytes 196616 | tf_op jit(solution)/shard_map/ppermute | solution.py:553
  89.5 10.2 %collective-permute-start.29 = (bf16[256,512]{1,0:T(8,128)(2,1)S(1)}, bf16[256,512]{1,0:T(8,128)(2,1)S(1)}, u32[]{:S(2)}, u32[]{:S(2)}) collective-permute-start(bf16[256,512]{1,0:T(8,128)(2,1)S(1)} %get-tuple-element.49), channel_id=1, source_target_pairs={{0,4},{4,0},{8,12},{12,8},{16,20},{20,16},{24,28},{28,24},{1,5},{5... | collective-permute-start | bytes 786440 | tf_op jit(solution)/shard_map/ppermute | solution.py:53
  91.6 11.8 %collective-permute-start.28 = (bf16[4,256,256]{2,1,0:T(8,128)(2,1)S(1)}, bf16[4,256,256]{2,1,0:T(8,128)(2,1)S(1)}, u32[]{:S(2)}, u32[]{:S(2)}) collective-permute-start(bf16[4,256,256]{2,1,0:T(8,128)(2,1)S(1)} %xsplit.1), channel_id=1, source_target_pairs={{0,4},{4,0},{8,12},{12,8},{16,20},{20,16},{24,28},{28,24},{1,5},{5... | collective-permute-start | bytes 1572872 | tf_op jit(solution)/shard_map/ppermute | solution.py:53
  99.7 17.4 %collective-permute-start.30 = (bf16[512,256]{1,0:T(8,128)(2,1)S(1)}, bf16[512,256]{1,0:T(8,128)(2,1)S(1)}, u32[]{:S(2)}, u32[]{:S(2)}) collective-permute-start(bf16[512,256]{1,0:T(8,128)(2,1)S(1)} %pad_maximum_fusion.1), channel_id=1, source_target_pairs={{0,8},{4,12},{8,0},{12,4},{16,24},{20,28},{24,16},{28,20},{1,9},{5... | collective-permute-start | bytes 786440 | tf_op jit(solution)/shard_map/ppermute | solution.py:53
  100.0 19.8 %collective-permute-start.31 = (bf16[512,256]{1,0:T(8,128)(2,1)S(1)}, bf16[512,256]{1,0:T(8,128)(2,1)S(1)}, u32[]{:S(2)}, u32[]{:S(2)}) collective-permute-start(bf16[512,256]{1,0:T(8,128)(2,1)S(1)} %pad_maximum_fusion.refs_0_), channel_id=1, source_target_pairs={{0,16},{4,20},{8,24},{12,28},{16,0},{20,4},{24,8},{28,12},{1,17},{... | collective-permute-start | bytes 786440 | tf_op jit(solution)/shard_map/ppermute | solution.py:53
  100.0 19.7 %collective-permute-start.32 = (bf16[512,256]{1,0:T(8,128)(2,1)S(1)}, bf16[512,256]{1,0:T(8,128)(2,1)S(1)}, u32[]{:S(2)}, u32[]{:S(2)}) collective-permute-start(bf16[512,256]{1,0:T(8,128)(2,1)S(1)} %pad_maximum_fusion.1), channel_id=1, source_target_pairs={{0,24},{4,28},{8,16},{12,20},{16,8},{20,12},{24,0},{28,4},{1,25},{... | collective-permute-start | bytes 786440 | tf_op jit(solution)/shard_map/ppermute | solution.py:53
  115.7 12.1 %collective-permute-start.33 = (bf16[128,256]{1,0:T(8,128)(2,1)S(1)}, bf16[128,256]{1,0:T(8,128)(2,1)S(1)}, u32[]{:S(2)}, u32[]{:S(2)}) collective-permute-start(bf16[128,256]{1,0:T(8,128)(2,1)S(1)} %get-tuple-element.52), channel_id=1, source_target_pairs={{0,16},{4,20},{8,24},{12,28},{1,17},{5,21},{9,25},{13,29},{2,18},{... | collective-permute-start | bytes 196616 | tf_op jit(solution)/shard_map/ppermute | solution.py:744
  (21 other events, 527.2 us)

commit v3 on v2

--- a/solution.py
+++ b/solution.py
@@ -299,6 +299,23 @@
     return mixed / (1.0 + jnp.exp(-mixed))
 
 
+def three_parts(values):
+    high = values.astype(BF16)
+    rest = values - high.astype(F32)
+    middle = rest.astype(BF16)
+    low = (rest - middle.astype(F32)).astype(BF16)
+    return high, middle, low
+
+
+def over_lanes(by_head, heads):
+    return lax.dot_general(
+        jnp.concatenate(three_parts(by_head), axis=0),
+        jnp.concatenate([heads] * 3, axis=0).astype(BF16),
+        (((0,), (0,)), ((), ())),
+        preferred_element_type=F32,
+    )
+
+
 def spread(width):
     row = lax.broadcasted_iota(jnp.int32, (PAD, width), 0)
     column = lax.broadcasted_iota(jnp.int32, (PAD, width), 1)
@@ -351,14 +368,15 @@
     logdec = (step * rate[...][None]).reshape(total, SPAN)
     row = lax.broadcasted_iota(jnp.int32, (SPAN, SPAN), 0)
     column = lax.broadcasted_iota(jnp.int32, (SPAN, SPAN), 1)
-    upper = (row <= column).astype(F32)
-    cum_out[...] = exact_dot(logdec, upper, ((1,), (0,))).reshape(step_out.shape)
+    upper = (row <= column).astype(BF16)
+    parts = jnp.concatenate(three_parts(logdec), axis=1)
+    cum_out[...] = wide_dot(parts, jnp.concatenate([upper] * 3, axis=0)).reshape(step_out.shape)
 
     def one(p, _):
         half_out[pl.ds(pl.multiple_of(p * SPAN, SPAN), SPAN), :] = convolved(pre, taps, p).astype(BF16)
         return 0
 
-    lax.fori_loop(0, step_out.shape[0], one, 0, unroll=2)
+    lax.fori_loop(0, step_out.shape[0], one, 0, unroll=16)
 
 
 def mixer_kernel(inner_count, shared, z_count, place, taps, half, half_other, step, cum, other, *refs):
@@ -400,14 +418,14 @@
         cum_p = cum[p]
         ends = cum_p[:, SPAN - 1 :]
         to_end = jnp.exp(ends - cum_p) * step[p]
-        scaled = (x.astype(F32) * exact_dot(to_end, heads, ((0,), (0,)))).astype(BF16)
+        scaled = (x.astype(F32) * over_lanes(to_end, heads)).astype(BF16)
         b = jnp.where(core == 0, half[rows, :], half_other[rows, :])
         fresh = lax.dot_general(b, scaled, (((0,), (0,)), ((), ())), preferred_element_type=F32)
         end_row = jnp.sum(ends * heads, axis=0, keepdims=True)
         return jnp.exp(end_row) * state + fresh, log_sum + end_row
 
     state, log_sum = lax.fori_loop(
-        0, step.shape[0], one, (jnp.zeros((N, width), F32), jnp.zeros((1, width), F32)), unroll=2
+        0, step.shape[0], one, (jnp.zeros((N, width), F32), jnp.zeros((1, width), F32)), unroll=16
     )
     last_out[...] = state.astype(BF16)
     through_out[...] = jnp.broadcast_to(jnp.exp(log_sum), through_out.shape)
@@ -468,13 +486,13 @@
             parts.append(jnp.where(lane == h, x, jnp.zeros_like(x)))
         diagonal = wide_dot(jnp.concatenate(mixes, axis=1), jnp.concatenate(parts, axis=0))
         state = states[p] + jnp.exp(before) * entering
-        decay = exact_dot(jnp.exp(cum_p), heads, ((0,), (0,)))
+        decay = over_lanes(jnp.exp(cum_p), heads)
         y = diagonal + decay * wide_dot(c, state.astype(BF16))
         g = gate[rows, :].astype(F32)
         gated_out[rows, :] = (y * (g / (1.0 + jnp.exp(-g)))).astype(BF16)
         return before + jnp.sum(cum_p[:, SPAN - 1 :] * heads, axis=0, keepdims=True)
 
-    lax.fori_loop(0, step.shape[0], one, jnp.zeros((1, width), F32), unroll=2)
+    lax.fori_loop(0, step.shape[0], one, jnp.zeros((1, width), F32), unroll=16)
 
 
 def norm_kernel(inner_count, parts, gain, out):

time: 160 us -> 157 us (0.981)
  Pallas kernels: 35.6 us -> 27.1 us
  waiting for transfers between devices: 45.5 us -> 50.9 us
    ppermute x29, waiting for transfers between devices: 31.1 us -> 37.8 us  [swapped(): return lax.ppermute(x, axis, pairs)]
    pallas_call x1, Pallas kernels: 12.3 us -> 6.75 us  [on_device(): pl.pallas_call(at(functools.partial(mixer_kernel, inner_count, shared, z_...]
    pallas_call x1, Pallas kernels: 6.03 us -> 3.21 us  [on_device(): pl.pallas_call(at(scan_kernel), in_specs=[VMEM] * 8, out_specs=VMEM, out_...]
  transfers between devices with their start and end apart: 34 -> 34, of which waited for: 10 -> 10; matrix products, arithmetic and copies ran while one was open for 0% -> 0% of each run, Pallas kernels for 18% -> 15%
where the time goes in v3:
time: 157 us; the launch traced here: 155 us
  waiting for transfers between devices  50.9 us (32%)
  starting transfers between devices  50.1 us (32%)
  Pallas kernels  27.1 us (17%)
  blocking collectives  22.6 us (14%)
  local copies, waits for them, and re-layouts  3.91 us (2%)
    ppermute x29, starting transfers between devices, swapped(): return lax.ppermute(x, axis, pairs)  45.1 us
    ppermute x29, waiting for transfers between devices, swapped(): return lax.ppermute(x, axis, pairs)  37.8 us
    all_to_all x1, blocking collectives, on_device(): lax.all_to_all(gated, ('ctx', 'inner'), 0, 0, axis_index_groups=teams, ti...  22.6 us
    pallas_call x1, Pallas kernels, on_device(): pl.pallas_call(at(functools.partial(state_kernel, inner_count)), in_specs...  7.22 us
    pallas_call x1, Pallas kernels, on_device(): pl.pallas_call(at(functools.partial(mixer_kernel, inner_count, shared, z_...  6.75 us
    ppermute x2, waiting for transfers between devices, inner_blocks(): far = lax.ppermute(onward, ('ctx', 'inner'), pairs)  5.64 us
    ppermute x2, waiting for transfers between devices, on_device(): halo = halo + lax.ppermute(tail, 'ctx', pairs)  4.64 us
    pallas_call x1, Pallas kernels, on_device(): pl.pallas_call(at(functools.partial(gate_kernel, inner_count, shared, z_c...  3.95 us
  transfers between devices with their start and end apart: 34, of which 10 were waited for; matrix products, arithmetic and copies ran while one was open for 0% of the time, Pallas kernels for 15%

profile of v3, /device:TPU:25, one launch (start us, length us, event | category | flops | bytes accessed | tf_op | source)
XLA Modules:
  0.0 155.0 jit_solution(15449771635728149215)
XLA Ops:
  2.6 10.4 %collective-permute-done.14.refs_12_ = bf16[128,2048]{1,0:T(8,128)(2,1)S(1)} collective-permute-done((bf16[128,2048]{1,0:T(8,128)(2,1)}, bf16[128,2048]{1,0:T(8,128)(2,1)S(1)}, u32[]{:S(2)}, u32[]{:S(2)}) %collective-permute-start.14) | collective-permute-done | bytes 524320 | tf_op jit(solution)/shard_map/ppermute | solution.py:53
  18.1 7.5 %collective-permute-done.refs_1_ = bf16[64,256]{1,0:T(8,128)(2,1)S(1)} collective-permute-done((bf16[64,256]{1,0:T(8,128)(2,1)S(1)}, bf16[64,256]{1,0:T(8,128)(2,1)S(1)}, u32[]{:S(2)}, u32[]{:S(2)}) %collective-permute-start) | collective-permute-done | bytes 32800 | tf_op jit(solution)/shard_map/ppermute | solution.py:53
  26.9 1.5 collective-permute-done.1.refs_2_
  28.4 2.2 %collective-permute-start.2 = (bf16[64,256]{1,0:T(8,128)(2,1)S(1)}, bf16[64,256]{1,0:T(8,128)(2,1)S(1)}, u32[]{:S(2)}, u32[]{:S(2)}) collective-permute-start(bf16[64,256]{1,0:T(8,128)(2,1)S(1)} %get-tuple-element.35), channel_id=1, source_target_pairs={{0,3},{1,2},{2,1},{3,0},{4,7},{5,6},{6,5},{7,4},{8,11},{9,10},{10,... | collective-permute-start | bytes 98312 | tf_op jit(solution)/shard_map/ppermute | solution.py:53
  33.8 4.6 %collective-permute-done.4.refs_2_.refs_3_ = bf16[264,256]{1,0:T(8,128)(2,1)S(1)} collective-permute-done((bf16[264,256]{1,0:T(8,128)(2,1)S(1)}, bf16[264,256]{1,0:T(8,128)(2,1)S(1)}, u32[]{:S(2)}, u32[]{:S(2)}) %collective-permute-start.4) | collective-permute-done | bytes 135200 | tf_op jit(solution)/shard_map/ppermute | solution.py:53
  41.4 2.7 %collective-permute-done.5.refs_3_.refs_4_ = bf16[264,256]{1,0:T(8,128)(2,1)S(1)} collective-permute-done((bf16[264,256]{1,0:T(8,128)(2,1)S(1)}, bf16[264,256]{1,0:T(8,128)(2,1)S(1)}, u32[]{:S(2)}, u32[]{:S(2)}) %collective-permute-start.5) | collective-permute-done | bytes 135200 | tf_op jit(solution)/shard_map/ppermute | solution.py:53
  44.2 2.7 %collective-permute-start.25 = (bf16[256,512]{1,0:T(8,128)(2,1)S(1)}, bf16[256,512]{1,0:T(8,128)(2,1)S(1)}, u32[]{:S(2)}, u32[]{:S(2)}) collective-permute-start(bf16[256,512]{1,0:T(8,128)(2,1)S(1)} %get-tuple-element.45), channel_id=1, source_target_pairs={{0,8},{4,12},{8,0},{12,4},{16,24},{20,28},{24,16},{28,20},{1,9},{5... | collective-permute-start | bytes 786440 | tf_op jit(solution)/shard_map/ppermute | solution.py:53
  46.9 3.1 %collective-permute-start.27 = (bf16[256,512]{1,0:T(8,128)(2,1)S(1)}, bf16[256,512]{1,0:T(8,128)(2,1)S(1)}, u32[]{:S(2)}, u32[]{:S(2)}) collective-permute-start(bf16[256,512]{1,0:T(8,128)(2,1)S(1)} %get-tuple-element.45), channel_id=1, source_target_pairs={{0,24},{4,28},{8,16},{12,20},{16,8},{20,12},{24,0},{28,4},{1,25},{... | collective-permute-start | bytes 786440 | tf_op jit(solution)/shard_map/ppermute | solution.py:53
  50.0 8.3 %collective-permute-start.10 = (bf16[128,2048]{1,0:T(8,128)(2,1)}, bf16[128,2048]{1,0:T(8,128)(2,1)S(1)}, u32[]{:S(2)}, u32[]{:S(2)}) collective-permute-start(bf16[128,2048]{1,0:T(8,128)(2,1)} %refs_4_.1), channel_id=1, source_target_pairs={{0,4},{4,0},{8,12},{12,8},{16,20},{20,16},{24,28},{28,24},{1,5},{5... | collective-permute-start | bytes 1572872 | tf_op jit(solution)/shard_map/ppermute | solution.py:53
  58.4 10.3 %collective-permute-start.11 = (bf16[128,2048]{1,0:T(8,128)(2,1)S(1)}, bf16[128,2048]{1,0:T(8,128)(2,1)S(1)}, u32[]{:S(2)}, u32[]{:S(2)}) collective-permute-start(bf16[128,2048]{1,0:T(8,128)(2,1)S(1)} %collective-permute-done.7.refs_0_.refs_1_.refs_5_), channel_id=1, source_target_pairs={{0,4},{4,0},{8,12},{12,8},{16,20},{20,16},{24,28},{28,24},{1,5},{5... | collective-permute-start | bytes 1572872 | tf_op jit(solution)/shard_map/ppermute | solution.py:53
  69.9 2.0 %collective-permute-start.6 = (bf16[4,136,256]{2,1,0:T(8,128)(2,1)S(1)}, bf16[4,136,256]{2,1,0:T(8,128)(2,1)S(1)}, u32[]{:S(2)}, u32[]{:S(2)}) collective-permute-start(bf16[4,136,256]{2,1,0:T(8,128)(2,1)S(1)} %ssplit.1), channel_id=1, source_target_pairs={{0,4},{4,0},{8,12},{12,8},{16,20},{20,16},{24,28},{28,24},{1,5},{5... | collective-permute-start | bytes 835592 | tf_op jit(solution)/shard_map/ppermute | solution.py:53
  72.5 5.6 %collective-permute-done.17.refs_15_ = bf16[128,2048]{1,0:T(8,128)(2,1)S(1)} collective-permute-done((bf16[128,2048]{1,0:T(8,128)(2,1)S(1)}, bf16[128,2048]{1,0:T(8,128)(2,1)S(1)}, u32[]{:S(2)}, u32[]{:S(2)}) %collective-permute-start.17) | collective-permute-done | bytes 524320 | tf_op jit(solution)/shard_map/ppermute | solution.py:79
  82.8 2.0 %settings.1 = (bf16[256,256]{1,0:T(8,128)(2,1)S(1)}, bf16[256,256]{1,0:T(8,128)(2,1)S(1)}, bf16[256,512]{1,0:T(8,128)(2,1)S(1)}, f32[8,128]{1,0:T(8,128)S(1)}, f...) custom-call(bf16[256,2,1024]{2,1,0:T(2,128)(2,1)S(1)} %copy-done.1, f32[5,2,512]{2,1,0:T(2,128)S(1)} %copy-done.6, ...), custom_call_target="tpu_custom_call" | custom-call | tf_op jit(solution)/shard_map/settings/pallas_call | solution.py:613
  84.8 4.6 %collective-permute-done.23 = bf16[16,2048]{1,0:T(8,128)(2,1)S(1)} collective-permute-done((bf16[16,2048]{1,0:T(8,128)(2,1)S(1)}, bf16[16,2048]{1,0:T(8,128)(2,1)S(1)}, u32[]{:S(2)}, u32[]{:S(2)}) %collective-permute-start.23) | collective-permute-done | bytes 65568 | tf_op jit(solution)/shard_map/ppermute | solution.py:571
  89.5 1.7 %collective-permute-start.29 = (bf16[256,512]{1,0:T(8,128)(2,1)S(1)}, bf16[256,512]{1,0:T(8,128)(2,1)S(1)}, u32[]{:S(2)}, u32[]{:S(2)}) collective-permute-start(bf16[256,512]{1,0:T(8,128)(2,1)S(1)} %get-tuple-element.49), channel_id=1, source_target_pairs={{0,4},{4,0},{8,12},{12,8},{16,20},{20,16},{24,28},{28,24},{1,5},{5... | collective-permute-start | bytes 786440 | tf_op jit(solution)/shard_map/ppermute | solution.py:53
  91.7 7.2 %state.1 = (bf16[2048,128]{1,0:T(8,128)(2,1)S(1)}, f32[16,8,128]{2,1,0:T(8,128)S(1)}, f32[16,8,128]{2,1,0:T(8,128)S(1)}, bf16[2064,2048]{1,0:T(8,128)(2,1)S(1)}) custom-call(f32[8,128]{1,0:T(8,128)S(1)} %get-tuple-element.29.refs_0_, f32[8,128]{1,0:T(8,128)S(1)} %get-tuple-element.30.refs_1_, f32[8,128]{1,0:T(8,128)S(1)} %get-tuple-element.31.refs_2_, ...), custom_call_target="tpu_custom_call" | custom-call | tf_op jit(solution)/shard_map/state/pallas_call | solution.py:725
  99.9 3.4 %collective-permute-start.32 = (bf16[512,256]{1,0:T(8,128)(2,1)S(1)}, bf16[512,256]{1,0:T(8,128)(2,1)S(1)}, u32[]{:S(2)}, u32[]{:S(2)}) collective-permute-start(bf16[512,256]{1,0:T(8,128)(2,1)S(1)} %pad_maximum_fusion.1), channel_id=1, source_target_pairs={{0,24},{4,28},{8,16},{12,20},{16,8},{20,12},{24,0},{28,4},{1,25},{... | collective-permute-start | bytes 786440 | tf_op jit(solution)/shard_map/ppermute | solution.py:53
  103.3 6.7 %mixer.1 = (bf16[2048,256]{1,0:T(8,128)(2,1)S(1)}, f32[16,128,256]{2,1,0:T(8,128)S(1)}, bf16[128,256]{1,0:T(8,128)(2,1)S(1)}, f32[8,256]{1,0:T(8,128)}) custom-call(f32[8,256]{1,0:T(8,128)S(1)} %get-tuple-element.41.refs_0_, bf16[2048,128]{1,0:T(8,128)(2,1)S(1)} %get-tuple-element.40.refs_1_.refs_0_, ...), custom_call_target="tpu_custom_call" | custom-call | tf_op jit(solution)/shard_map/mixer/pallas_call | solution.py:740
  110.0 1.5 collective-permute-start.33
  111.6 9.5 %collective-permute-done.31.refs_2_ = bf16[512,256]{1,0:T(8,128)(2,1)S(1)} collective-permute-done((bf16[512,256]{1,0:T(8,128)(2,1)S(1)}, bf16[512,256]{1,0:T(8,128)(2,1)S(1)}, u32[]{:S(2)}, u32[]{:S(2)}) %collective-permute-start.31) | collective-permute-done | bytes 262176 | tf_op jit(solution)/shard_map/ppermute | solution.py:53
  121.0 4.0 %gate.1.refs_3_ = bf16[2048,256]{1,0:T(8,128)(2,1)S(1)} custom-call(bf16[512,256]{1,0:T(8,128)(2,1)S(1)} %pad_maximum_fusion.refs_0_, bf16[512,256]{1,0:T(8,128)(2,1)S(1)} %collective-permute-done.30.refs_1_, bf16[512,256]{1,0:T(8,128)(2,1)S(1)} %collective-permute-done.31.refs_2_, bf16[512,256]{1,0:T(8,128)(2,1)S(1)} %collective-permute-done.32.refs_3_, ...), custom_call_target="tpu_custom_call" | custom-call | tf_op jit(solution)/shard_map/gate/pallas_call | solution.py:764
  125.0 2.8 %collective-permute-done.33.refs_7_ = bf16[128,256]{1,0:T(8,128)(2,1)S(1)} collective-permute-done((bf16[128,256]{1,0:T(8,128)(2,1)S(1)}, bf16[128,256]{1,0:T(8,128)(2,1)S(1)}, u32[]{:S(2)}, u32[]{:S(2)}) %collective-permute-start.33) | collective-permute-done | bytes 65568 | tf_op jit(solution)/shard_map/ppermute | solution.py:762
  127.8 3.2 %scan.1 = bf16[2048,256]{1,0:T(8,128)(2,1)S(1)} custom-call(bf16[2048,128]{1,0:T(8,128)(2,1)S(1)} %get-tuple-element.40.refs_1_.refs_0_, bf16[2048,128]{1,0:T(8,128)(2,1)S(1)} %collective-permute-done.24.refs_2_.refs_1_, bf16[2048,256]{1,0:T(8,128)(2,1)S(1)} %get-tuple-element.47.refs_2_, bf16[2048,256]{1,0:T(8,128)(2,1)S(1)} %gate.1.refs_3_, ...), custom_call_target="tpu_custom_call" | custom-call | tf_op jit(solution)/shard_map/scan/pallas_call | solution.py:774
  131.0 22.6 %all_to_all.9.refs_0_ = bf16[16,128,256]{2,1,0:T(8,128)(2,1)S(1)} all-to-all(bf16[16,128,256]{2,1,0:T(8,128)(2,1)S(1)} %bitcast.5), channel_id=1, replica_groups={{0,1,2,3,4,5,6,7,8,9,10,11,12,13,14,15},{16,17,18,19,20,21,22,23,24,25,..., dimensions={0} | all-to-all | bytes 2097152 | tf_op jit(solution)/shard_map/all_to_all | solution.py:784
  (87 shorter events, 24.5 us)
Async XLA Ops:
  0.0 13.0 %collective-permute-start.14 = (bf16[128,2048]{1,0:T(8,128)(2,1)}, bf16[128,2048]{1,0:T(8,128)(2,1)S(1)}, u32[]{:S(2)}, u32[]{:S(2)}) collective-permute-start(bf16[128,2048]{1,0:T(8,128)(2,1)} %refs_4_.1), channel_id=1, source_target_pairs={{0,8},{4,12},{8,0},{12,4},{16,24},{20,28},{24,16},{28,20},{1,9},{5... | collective-permute-start | bytes 1572872 | tf_op jit(solution)/shard_map/ppermute | solution.py:53
  0.2 32.1 %collective-permute-start.7 = (bf16[128,2048]{1,0:T(8,128)(2,1)}, bf16[128,2048]{1,0:T(8,128)(2,1)S(1)}, u32[]{:S(2)}, u32[]{:S(2)}) collective-permute-start(bf16[128,2048]{1,0:T(8,128)(2,1)} %refs_4_.1), channel_id=1, source_target_pairs={{0,1},{1,0},{2,3},{3,2},{4,5},{5,4},{6,7},{7,6},{8,9},{9,8},{10,11... | collective-permute-start | bytes 1572872 | tf_op jit(solution)/shard_map/ppermute | solution.py:53
  1.4 30.9 %collective-permute-start.8 = (bf16[128,2048]{1,0:T(8,128)(2,1)}, bf16[128,2048]{1,0:T(8,128)(2,1)S(1)}, u32[]{:S(2)}, u32[]{:S(2)}) collective-permute-start(bf16[128,2048]{1,0:T(8,128)(2,1)} %refs_4_.1), channel_id=1, source_target_pairs={{0,2},{1,3},{2,0},{3,1},{4,6},{5,7},{6,4},{7,5},{8,10},{9,11},{10,... | collective-permute-start | bytes 1572872 | tf_op jit(solution)/shard_map/ppermute | solution.py:53
  13.0 33.8 %collective-permute-start.15 = (bf16[128,2048]{1,0:T(8,128)(2,1)S(1)}, bf16[128,2048]{1,0:T(8,128)(2,1)S(1)}, u32[]{:S(2)}, u32[]{:S(2)}) collective-permute-start(bf16[128,2048]{1,0:T(8,128)(2,1)S(1)} %collective-permute-done.14.refs_12_), channel_id=1, source_target_pairs={{0,1},{1,0},{2,3},{3,2},{4,5},{5,4},{6,7},{7,6},{8,9},{9,8},{10,11... | collective-permute-start | bytes 1572872 | tf_op jit(solution)/shard_map/ppermute | solution.py:53
  14.2 35.7 %collective-permute-start.16 = (bf16[128,2048]{1,0:T(8,128)(2,1)S(1)}, bf16[128,2048]{1,0:T(8,128)(2,1)S(1)}, u32[]{:S(2)}, u32[]{:S(2)}) collective-permute-start(bf16[128,2048]{1,0:T(8,128)(2,1)S(1)} %collective-permute-done.14.refs_12_), channel_id=1, source_target_pairs={{0,2},{1,3},{2,0},{3,1},{4,6},{5,7},{6,4},{7,5},{8,10},{9,11},{10,... | collective-permute-start | bytes 1572872 | tf_op jit(solution)/shard_map/ppermute | solution.py:53
  32.3 37.5 %collective-permute-start.9 = (bf16[128,2048]{1,0:T(8,128)(2,1)S(1)}, bf16[128,2048]{1,0:T(8,128)(2,1)S(1)}, u32[]{:S(2)}, u32[]{:S(2)}) collective-permute-start(bf16[128,2048]{1,0:T(8,128)(2,1)S(1)} %either.2), channel_id=1, source_target_pairs={{0,2},{1,3},{2,0},{3,1},{4,5},{5,4},{6,7},{7,6},{8,10},{9,11},{10,... | collective-permute-start | bytes 1572872 | tf_op jit(solution)/shard_map/ppermute | solution.py:79
  41.4 17.0 %collective-permute-start.26 = (bf16[256,512]{1,0:T(8,128)(2,1)S(1)}, bf16[256,512]{1,0:T(8,128)(2,1)S(1)}, u32[]{:S(2)}, u32[]{:S(2)}) collective-permute-start(bf16[256,512]{1,0:T(8,128)(2,1)S(1)} %get-tuple-element.44.refs_0_.refs_6_), channel_id=1, source_target_pairs={{0,16},{4,20},{8,24},{12,28},{16,0},{20,4},{24,8},{28,12},{1,17},{... | collective-permute-start | bytes 786440 | tf_op jit(solution)/shard_map/ppermute | solution.py:53
  44.2 24.5 %collective-permute-start.25 = (bf16[256,512]{1,0:T(8,128)(2,1)S(1)}, bf16[256,512]{1,0:T(8,128)(2,1)S(1)}, u32[]{:S(2)}, u32[]{:S(2)}) collective-permute-start(bf16[256,512]{1,0:T(8,128)(2,1)S(1)} %get-tuple-element.45), channel_id=1, source_target_pairs={{0,8},{4,12},{8,0},{12,4},{16,24},{20,28},{24,16},{28,20},{1,9},{5... | collective-permute-start | bytes 786440 | tf_op jit(solution)/shard_map/ppermute | solution.py:53
  46.9 22.9 %collective-permute-start.27 = (bf16[256,512]{1,0:T(8,128)(2,1)S(1)}, bf16[256,512]{1,0:T(8,128)(2,1)S(1)}, u32[]{:S(2)}, u32[]{:S(2)}) collective-permute-start(bf16[256,512]{1,0:T(8,128)(2,1)S(1)} %get-tuple-element.45), channel_id=1, source_target_pairs={{0,24},{4,28},{8,16},{12,20},{16,8},{20,12},{24,0},{28,4},{1,25},{... | collective-permute-start | bytes 786440 | tf_op jit(solution)/shard_map/ppermute | solution.py:53
  50.0 19.9 %collective-permute-start.10 = (bf16[128,2048]{1,0:T(8,128)(2,1)}, bf16[128,2048]{1,0:T(8,128)(2,1)S(1)}, u32[]{:S(2)}, u32[]{:S(2)}) collective-permute-start(bf16[128,2048]{1,0:T(8,128)(2,1)} %refs_4_.1), channel_id=1, source_target_pairs={{0,4},{4,0},{8,12},{12,8},{16,20},{20,16},{24,28},{28,24},{1,5},{5... | collective-permute-start | bytes 1572872 | tf_op jit(solution)/shard_map/ppermute | solution.py:53
  58.4 13.6 %collective-permute-start.11 = (bf16[128,2048]{1,0:T(8,128)(2,1)S(1)}, bf16[128,2048]{1,0:T(8,128)(2,1)S(1)}, u32[]{:S(2)}, u32[]{:S(2)}) collective-permute-start(bf16[128,2048]{1,0:T(8,128)(2,1)S(1)} %collective-permute-done.7.refs_0_.refs_1_.refs_5_), channel_id=1, source_target_pairs={{0,4},{4,0},{8,12},{12,8},{16,20},{20,16},{24,28},{28,24},{1,5},{5... | collective-permute-start | bytes 1572872 | tf_op jit(solution)/shard_map/ppermute | solution.py:53
  69.8 8.4 %collective-permute-start.17 = (bf16[128,2048]{1,0:T(8,128)(2,1)S(1)}, bf16[128,2048]{1,0:T(8,128)(2,1)S(1)}, u32[]{:S(2)}, u32[]{:S(2)}) collective-permute-start(bf16[128,2048]{1,0:T(8,128)(2,1)S(1)} %either.3), channel_id=1, source_target_pairs={{0,2},{1,3},{2,0},{3,1},{4,5},{5,4},{6,7},{7,6},{8,10},{9,11},{10,... | collective-permute-start | bytes 1572872 | tf_op jit(solution)/shard_map/ppermute | solution.py:79
  69.9 10.7 %collective-permute-start.6 = (bf16[4,136,256]{2,1,0:T(8,128)(2,1)S(1)}, bf16[4,136,256]{2,1,0:T(8,128)(2,1)S(1)}, u32[]{:S(2)}, u32[]{:S(2)}) collective-permute-start(bf16[4,136,256]{2,1,0:T(8,128)(2,1)S(1)} %ssplit.1), channel_id=1, source_target_pairs={{0,4},{4,0},{8,12},{12,8},{16,20},{20,16},{24,28},{28,24},{1,5},{5... | collective-permute-start | bytes 835592 | tf_op jit(solution)/shard_map/ppermute | solution.py:53
  71.9 19.7 %collective-permute-start.18 = (bf16[128,2048]{1,0:T(8,128)(2,1)S(1)}, bf16[128,2048]{1,0:T(8,128)(2,1)S(1)}, u32[]{:S(2)}, u32[]{:S(2)}) collective-permute-start(bf16[128,2048]{1,0:T(8,128)(2,1)S(1)} %collective-permute-done.14.refs_12_), channel_id=1, source_target_pairs={{0,4},{4,0},{8,12},{12,8},{16,20},{20,16},{24,28},{28,24},{1,5},{5... | collective-permute-start | bytes 1572872 | tf_op jit(solution)/shard_map/ppermute | solution.py:53
  72.0 19.7 %collective-permute-start.19 = (bf16[128,2048]{1,0:T(8,128)(2,1)S(1)}, bf16[128,2048]{1,0:T(8,128)(2,1)S(1)}, u32[]{:S(2)}, u32[]{:S(2)}) collective-permute-start(bf16[128,2048]{1,0:T(8,128)(2,1)S(1)} %collective-permute-done.15.refs_0_.refs_13_), channel_id=1, source_target_pairs={{0,4},{4,0},{8,12},{12,8},{16,20},{20,16},{24,28},{28,24},{1,5},{5... | collective-permute-start | bytes 1572872 | tf_op jit(solution)/shard_map/ppermute | solution.py:53
  72.5 19.2 %collective-permute-start.20 = (bf16[128,2048]{1,0:T(8,128)(2,1)S(1)}, bf16[128,2048]{1,0:T(8,128)(2,1)S(1)}, u32[]{:S(2)}, u32[]{:S(2)}) collective-permute-start(bf16[128,2048]{1,0:T(8,128)(2,1)S(1)} %collective-permute-done.16.refs_1_.refs_14_), channel_id=1, source_target_pairs={{0,4},{4,0},{8,12},{12,8},{16,20},{20,16},{24,28},{28,24},{1,5},{5... | collective-permute-start | bytes 1572872 | tf_op jit(solution)/shard_map/ppermute | solution.py:53
  78.2 13.5 %collective-permute-start.21 = (bf16[128,2048]{1,0:T(8,128)(2,1)S(1)}, bf16[128,2048]{1,0:T(8,128)(2,1)S(1)}, u32[]{:S(2)}, u32[]{:S(2)}) collective-permute-start(bf16[128,2048]{1,0:T(8,128)(2,1)S(1)} %collective-permute-done.17.refs_15_), channel_id=1, source_target_pairs={{0,4},{4,0},{8,12},{12,8},{16,20},{20,16},{24,28},{28,24},{1,5},{5... | collective-permute-start | bytes 1572872 | tf_op jit(solution)/shard_map/ppermute | solution.py:53
  81.3 8.2 %collective-permute-start.23 = (bf16[16,2048]{1,0:T(8,128)(2,1)S(1)}, bf16[16,2048]{1,0:T(8,128)(2,1)S(1)}, u32[]{:S(2)}, u32[]{:S(2)}) collective-permute-start(bf16[16,2048]{1,0:T(8,128)(2,1)S(1)} %tail.1), channel_id=1, source_target_pairs={{8,24},{12,28},{9,25},{13,29},{10,26},{14,30},{11,27},{15,31}} | collective-permute-start | bytes 196616 | tf_op jit(solution)/shard_map/ppermute | solution.py:571
  89.5 10.0 %collective-permute-start.29 = (bf16[256,512]{1,0:T(8,128)(2,1)S(1)}, bf16[256,512]{1,0:T(8,128)(2,1)S(1)}, u32[]{:S(2)}, u32[]{:S(2)}) collective-permute-start(bf16[256,512]{1,0:T(8,128)(2,1)S(1)} %get-tuple-element.49), channel_id=1, source_target_pairs={{0,4},{4,0},{8,12},{12,8},{16,20},{20,16},{24,28},{28,24},{1,5},{5... | collective-permute-start | bytes 786440 | tf_op jit(solution)/shard_map/ppermute | solution.py:53
  91.6 11.6 %collective-permute-start.28 = (bf16[4,256,256]{2,1,0:T(8,128)(2,1)S(1)}, bf16[4,256,256]{2,1,0:T(8,128)(2,1)S(1)}, u32[]{:S(2)}, u32[]{:S(2)}) collective-permute-start(bf16[4,256,256]{2,1,0:T(8,128)(2,1)S(1)} %xsplit.1), channel_id=1, source_target_pairs={{0,4},{4,0},{8,12},{12,8},{16,20},{20,16},{24,28},{28,24},{1,5},{5... | collective-permute-start | bytes 1572872 | tf_op jit(solution)/shard_map/ppermute | solution.py:53
  99.6 12.0 %collective-permute-start.30 = (bf16[512,256]{1,0:T(8,128)(2,1)S(1)}, bf16[512,256]{1,0:T(8,128)(2,1)S(1)}, u32[]{:S(2)}, u32[]{:S(2)}) collective-permute-start(bf16[512,256]{1,0:T(8,128)(2,1)S(1)} %pad_maximum_fusion.1), channel_id=1, source_target_pairs={{0,8},{4,12},{8,0},{12,4},{16,24},{20,28},{24,16},{28,20},{1,9},{5... | collective-permute-start | bytes 786440 | tf_op jit(solution)/shard_map/ppermute | solution.py:53
  99.8 21.2 %collective-permute-start.31 = (bf16[512,256]{1,0:T(8,128)(2,1)S(1)}, bf16[512,256]{1,0:T(8,128)(2,1)S(1)}, u32[]{:S(2)}, u32[]{:S(2)}) collective-permute-start(bf16[512,256]{1,0:T(8,128)(2,1)S(1)} %pad_maximum_fusion.refs_0_), channel_id=1, source_target_pairs={{0,16},{4,20},{8,24},{12,28},{16,0},{20,4},{24,8},{28,12},{1,17},{... | collective-permute-start | bytes 786440 | tf_op jit(solution)/shard_map/ppermute | solution.py:53
  99.9 21.1 %collective-permute-start.32 = (bf16[512,256]{1,0:T(8,128)(2,1)S(1)}, bf16[512,256]{1,0:T(8,128)(2,1)S(1)}, u32[]{:S(2)}, u32[]{:S(2)}) collective-permute-start(bf16[512,256]{1,0:T(8,128)(2,1)S(1)} %pad_maximum_fusion.1), channel_id=1, source_target_pairs={{0,24},{4,28},{8,16},{12,20},{16,8},{20,12},{24,0},{28,4},{1,25},{... | collective-permute-start | bytes 786440 | tf_op jit(solution)/shard_map/ppermute | solution.py:53
  110.0 17.7 %collective-permute-start.33 = (bf16[128,256]{1,0:T(8,128)(2,1)S(1)}, bf16[128,256]{1,0:T(8,128)(2,1)S(1)}, u32[]{:S(2)}, u32[]{:S(2)}) collective-permute-start(bf16[128,256]{1,0:T(8,128)(2,1)S(1)} %get-tuple-element.52), channel_id=1, source_target_pairs={{0,16},{4,20},{8,24},{12,28},{1,17},{5,21},{9,25},{13,29},{2,18},{... | collective-permute-start | bytes 196616 | tf_op jit(solution)/shard_map/ppermute | solution.py:762
  (21 other events, 530.0 us)
